TPU v7x, 128 devices: a whole 4x4x4 slice. The times are simulated.
128 devices in a mesh: dp: 16 (over x_hi, z, core), space: 8 (over y, x_lo).
Axes of the slice: x: 4 (x_hi: 2, x_lo: 2; x = x_hi * 2 + x_lo), y: 4, z: 4, core: 2. Of those that a mesh axis runs over, the one named last changes fastest.
Arguments:
- inputs: bfloat16 [16, 24, 32, 32, 256], P('dp', 'space'), may hold values from -6 to 6
- kernels: bfloat16 [2, 3, 3, 256, 256], P(None, None, None, 'dp'), may hold values from -0.125 to 0.125
- cotangent: bfloat16 [16, 24, 32, 32, 256], P('dp', 'space'), may hold values from -0.01171875 to 0.01171875
- adjacency: int32 [24, 4, 3], P('space'), may hold values from 0 to 23, as said below
Outputs:
- final_state: bfloat16 [16, 24, 32, 32, 256], P('dp', 'space')
- kernel_grads: float32 [2, 3, 3, 256, 256], P(None, None, None, 'dp')
Inputs may be any that keep to these rules, and one draw needn't show every extreme that they name: Entry [t, e] = (n, f, r): edge e of tile t meets edge f of tile n, and r = 1 where the two edges are read in opposite directions along the shared line. The relation is symmetric: adjacency[n, f] = (t, e, r). The tiles form 2 x 2 blocks on the six faces of a cube, numbered in an order drawn from the seed.
All inputs are finite; a program needn't handle non-finite values.
Results may differ from a plain program's by a relative error of at most 0.005.
Values may be sent and summed in bfloat16 or wider, within the bound.
No kernel may reach another device: no remote copies, remote signals or barrier semaphores. Data moves between devices by JAX's collectives and lax.ppermute only.
A program may use at most 192 MiB of HBM per device.

v0:
```python
import jax
import jax.numpy as jnp
from jax import lax
from jax.sharding import PartitionSpec as P

LAYERS = 2


def copy_for_each(value, axis):
    count = lax.axis_size(axis)
    return lax.all_to_all(
        jnp.broadcast_to(value[None], (count, *value.shape)), axis, 0, 0, tiled=True
    )


def joined_along(blocks, dim):
    shape = list(blocks.shape[1:])
    shape[dim] *= blocks.shape[0]
    return jnp.moveaxis(blocks, 0, dim).reshape(shape)


def collect(value, axis, dim):
    blocks = copy_for_each(value, axis)
    return joined_along(blocks, dim)


def edge_strips(tile_field):
    return jnp.stack(
        [
            tile_field[:, :, 0],
            tile_field[:, :, -1],
            tile_field[:, :, :, 0],
            tile_field[:, :, :, -1],
        ],
        axis=2,
    )


def orient(strips, adjacency):
    selected = strips[:, adjacency[:, :, 0], adjacency[:, :, 1]]
    flipped = (adjacency[:, :, 2] == 1)[None, :, :, None, None]
    return jnp.where(flipped, selected[:, :, :, ::-1], selected)


def neighbor_rims(tile_field, adjacency):
    gathered = collect(edge_strips(tile_field), "space", 1)
    return orient(gathered, adjacency)


def returned_rims(rim_values, adjacency):
    gathered = collect(rim_values, "space", 1)
    return orient(gathered, adjacency)


def with_rim(tile_field, rim_rows):
    middle = jnp.concatenate(
        [rim_rows[:, :, 2][:, :, :, None], tile_field, rim_rows[:, :, 3][:, :, :, None]], axis=3
    )
    corner = jnp.zeros(tile_field.shape[:2] + (1, tile_field.shape[4]), tile_field.dtype)
    top_row = jnp.concatenate([corner, rim_rows[:, :, 0], corner], axis=2)[:, :, None]
    bottom_row = jnp.concatenate([corner, rim_rows[:, :, 1], corner], axis=2)[:, :, None]
    return jnp.concatenate([top_row, middle, bottom_row], axis=2)


def convolve(padded, kernel):
    extent = padded.shape[2] - 2
    channels = padded.shape[-1]
    summed = jnp.zeros(padded.shape[:2] + (extent, extent, kernel.shape[-1]), jnp.float32)
    for row_off in range(3):
        for col_off in range(3):
            patches = padded[:, :, row_off : row_off + extent, col_off : col_off + extent].reshape(
                -1, channels
            )
            summed = summed + jnp.dot(
                patches, kernel[row_off, col_off], preferred_element_type=jnp.float32
            ).reshape(summed.shape)
    return summed


def weight_grad(padded, flat_grad):
    extent = padded.shape[2] - 2
    channels = padded.shape[-1]
    rows_out = []
    for row_off in range(3):
        row_list = []
        for col_off in range(3):
            patches = padded[:, :, row_off : row_off + extent, col_off : col_off + extent].reshape(
                -1, channels
            )
            row_list.append(
                lax.dot_general(
                    patches, flat_grad, (((0,), (0,)), ((), ())), preferred_element_type=jnp.float32
                )
            )
        rows_out.append(jnp.stack(row_list))
    return jnp.stack(rows_out)


def input_grad(flat_grad, kernel, padded_shape):
    extent = padded_shape[2] - 2
    full = extent + 2
    channels = padded_shape[4]
    grid_grad = flat_grad.reshape(padded_shape[:2] + (extent, extent, flat_grad.shape[-1]))
    widened = jnp.pad(grid_grad, ((0, 0), (0, 0), (2, 2), (2, 2), (0, 0)))
    pad_grad = jnp.zeros(padded_shape, jnp.float32)
    for row_off in range(3):
        for col_off in range(3):
            window = widened[
                :, :, 2 - row_off : 2 - row_off + full, 2 - col_off : 2 - col_off + full
            ].reshape(-1, flat_grad.shape[-1])
            contrib = lax.dot_general(
                window,
                kernel[row_off, col_off],
                (((1,), (1,)), ((), ())),
                preferred_element_type=jnp.float32,
            )
            pad_grad = pad_grad + contrib.reshape(padded_shape[:4] + (channels,))
    return pad_grad


def rim_strips(pad_grad):
    return jnp.stack(
        [
            pad_grad[:, :, 0, 1:-1],
            pad_grad[:, :, -1, 1:-1],
            pad_grad[:, :, 1:-1, 0],
            pad_grad[:, :, 1:-1, -1],
        ],
        axis=2,
    )


def add_rim(interior, returned):
    interior = jnp.concatenate(
        [
            interior[:, :, :1] + returned[:, :, 0][:, :, None],
            interior[:, :, 1:-1],
            interior[:, :, -1:] + returned[:, :, 1][:, :, None],
        ],
        axis=2,
    )
    interior = jnp.concatenate(
        [
            interior[:, :, :, :1] + returned[:, :, 2][:, :, :, None],
            interior[:, :, :, 1:-1],
            interior[:, :, :, -1:] + returned[:, :, 3][:, :, :, None],
        ],
        axis=3,
    )
    return interior


def reduce_grad(partial_value):
    shard_part = lax.psum_scatter(partial_value, ("dp", "space"), scatter_dimension=2, tiled=True)
    return collect(shard_part, "space", 2)


def per_device(inputs, kernels, cotangent, adjacency):
    weights = lax.all_gather(kernels, "dp", axis=3, tiled=True)
    current = inputs
    stored = []
    for layer_num in range(LAYERS):
        padded = with_rim(current, neighbor_rims(current, adjacency))
        preact = convolve(padded, weights[layer_num])
        current = (current.astype(jnp.float32) + jax.nn.silu(preact)).astype(jnp.bfloat16)
        stored.append((padded, preact))
    upstream = cotangent.astype(jnp.float32)
    kernel_grads = [None] * LAYERS
    for layer_num in range(LAYERS - 1, -1, -1):
        padded, preact = stored[layer_num]
        logistic = jax.nn.sigmoid(preact)
        pre_grad = (upstream * logistic * (1.0 + preact * (1.0 - logistic))).astype(jnp.bfloat16)
        flat_grad = pre_grad.reshape(-1, pre_grad.shape[-1])
        kernel_grads[layer_num] = reduce_grad(weight_grad(padded, flat_grad))
        if layer_num > 0:
            pad_grad = input_grad(flat_grad, weights[layer_num], padded.shape)
            rim_values = rim_strips(pad_grad).astype(jnp.bfloat16)
            returned = returned_rims(rim_values, adjacency).astype(jnp.float32)
            upstream = add_rim(upstream + pad_grad[:, :, 1:-1, 1:-1], returned)
    return (current, jnp.stack(kernel_grads))


def solution(mesh):
    in_specs = (
        P("dp", "space", None, None, None),
        P(None, None, None, "dp", None),
        P("dp", "space", None, None, None),
        P("space", None, None),
    )
    out_specs = (P("dp", "space", None, None, None), P(None, None, None, "dp", None))
    return jax.shard_map(
        per_device, mesh=mesh, in_specs=in_specs, out_specs=out_specs, check_vma=False
    )
```

profile of v0, /device:TPU:0, one launch (start us, length us, event | category | flops | bytes accessed | tf_op | source)
XLA Modules:
  0.0 433.2 jit_solution(11384724083238640514)
XLA Ops:
  7.9 2.4 copy.309
  11.8 5.6 %all-to-all-start = ((bf16[8,1,3,4,32,256]{5,4,3,2,1,0:T(8,128)(2,1)}), bf16[8,1,3,4,32,256]{5,4,3,2,1,0:T(8,128)(2,1)S(1)}, u32[]{:S(2)}, u32[]{:S(2)}) async-start(bf16[8,1,3,4,32,256]{5,4,3,2,1,0:T(8,128)(2,1)} %broadcast_in_dim.38), calls=%async_computation | async-start | bytes 3145728 | tf_op jit(solution)/shard_map/all_to_all | solution.py:11
  17.9 22.4 %all-to-all-done = bf16[8,1,3,4,32,256]{5,4,3,2,1,0:T(8,128)(2,1)S(1)} async-done(((bf16[8,1,3,4,32,256]{5,4,3,2,1,0:T(8,128)(2,1)}), bf16[8,1,3,4,32,256]{5,4,3,2,1,0:T(8,128)(2,1)S(1)}, u32[]{:S(2)}, u32[]{:S(2)}) %all-to-all-start) | async-done | bytes 1572896 | tf_op jit(solution)/shard_map/all_to_all | solution.py:11
  41.5 3.1 fusion.35
  44.6 2.4 maximum_maximum_fusion.1
  49.0 5.0 %slice_bitcast_fusion.7 = (bf16[3,32,32,256]{3,2,1,0:T(8,128)(2,1)}, bf16[3,32,32,256]{3,2,1,0:T(8,128)(2,1)}, bf16[3,32,32,256]{3,2,1,0:T(8,128)(2,1)}, bf16[3,...) fusion(bf16[1,3,33,34,256]{4,3,2,1,0:T(8,128)(2,1)S(1)} %get-tuple-element.37, ...), kind=kLoop, calls=%fused_computation.63 | loop fusion | bytes 18874368 | tf_op jit(solution)/shard_map/dot_general | solution.py:74
  54.0 8.5 %all-gather.2.cloned.1.call-done = bf16[2,3,3,256,256]{4,3,2,1,0:T(8,128)(2,1)} async-done(((bf16[2,3,3,16,256]{4,3,2,1,0:T(8,128)(2,1)}), bf16[2,3,3,256,256]{4,3,2,1,0:T(8,128)(2,1)}) %all-gather.2.cloned.1.call-update) | async-done | bytes 2359312 | tf_op jit(solution)/shard_map/all_gather | solution.py:159
  62.6 2.9 slice_bitcast_fusion.14
  67.4 1.8 fusion.39
  69.2 1.8 fusion.41
  71.1 1.8 fusion.43
  72.9 1.8 fusion.45
  74.8 1.8 fusion.47
  76.6 3.7 fusion.51
  80.3 3.5 fusion.49
  83.8 10.0 %fusion.5 = (bf16[1,3,32,32,256]{4,2,1,3,0:T(8,128)(2,1)S(1)}, f32[3,32,32,256]{3,1,0,2:T(8,128)}) fusion(bf16[1,3,32,32,256]{4,3,2,1,0:T(8,128)(2,1)S(1)} %copy-done, bf16[3,3,256,256]{3,2,1,0:T(8,128)(2,1)} %copy-done.26, bf16[3,32,32,256]{3,2,1,0:T(8,128)(2,1)} %get-tuple-element.30, f32[3,32,32,256]{3,1,0,2:T(8,128)S(1)} %fusion.37, ...), kind=kOutput, calls=%fused_computation.15 | convolution fusion | flops 414449664 | bytes 33161216 | tf_op jit(solution)/shard_map/dot_general | solution.py:74
  95.4 4.9 %all-to-all-start.1 = ((bf16[8,1,3,4,32,256]{5,4,3,2,1,0:T(8,128)(2,1)}), bf16[8,1,3,4,32,256]{5,4,3,2,1,0:T(8,128)(2,1)}, u32[]{:S(2)}, u32[]{:S(2)}) async-start(bf16[8,1,3,4,32,256]{5,4,3,2,1,0:T(8,128)(2,1)} %broadcast_in_dim.75), calls=%async_computation.1 | async-start | bytes 3145728 | tf_op jit(solution)/shard_map/all_to_all | solution.py:11
  100.2 2.2 fusion.118
  102.4 19.8 %all-to-all-done.1 = bf16[8,1,3,4,32,256]{5,4,3,2,1,0:T(8,128)(2,1)} async-done(((bf16[8,1,3,4,32,256]{5,4,3,2,1,0:T(8,128)(2,1)}), bf16[8,1,3,4,32,256]{5,4,3,2,1,0:T(8,128)(2,1)}, u32[]{:S(2)}, u32[]{:S(2)}) %all-to-all-start.1) | async-done | bytes 1572896 | tf_op jit(solution)/shard_map/all_to_all | solution.py:11
  122.2 2.0 gather_fusion.1
  127.7 2.7 fusion.116
  130.4 2.3 fusion.114
  132.7 2.3 fusion.115
  135.0 3.6 slice_bitcast_fusion.3
  138.6 2.2 fusion.119
  140.8 2.2 fusion.117
  143.6 9.1 %fusion.1 = (bf16[1,3,32,32,256]{4,2,1,3,0:T(8,128)(2,1)S(1)}, bf16[1,3,32,32,256]{4,2,1,3,0:T(8,128)(2,1)}) fusion(bf16[1,3,32,32,256]{4,3,2,1,0:T(8,128)(2,1)} %param.6, bf16[1,3,32,32,256]{4,2,1,3,0:T(8,128)(2,1)S(1)} %get-tuple-element.66, bf16[3,3,256,256]{3,2,1,0:T(8,128)(2,1)} %get-tuple-element.19, ...), kind=kOutput, calls=%fused_computation.7 | convolution fusion | flops 419954688 | bytes 33161216 | tf_op jit(solution)/shard_map/dot_general | solution.py:74
  152.7 2.7 fusion.94
  158.1 2.4 slice_bitcast_fusion.6
  161.3 2.9 fusion.25
  164.1 2.8 fusion.22
  166.9 2.8 fusion.19
  169.7 2.9 fusion.16
  172.5 2.7 fusion.13
  175.2 2.7 fusion.7
  177.9 2.7 fusion.10
  180.7 12.9 %fusion.158 = (bf16[1,3,34,34,256]{4,2,1,3,0:T(8,128)(2,1)S(1)}, f32[1,3,34,34,256]{4,2,1,3,0:T(8,128)}) fusion(bf16[3,3,256,256]{3,2,1,0:T(8,128)(2,1)S(1)} %copy-done.15, bf16[1,3,32,32,256]{4,2,1,3,0:T(8,128)(2,1)S(1)} %get-tuple-element.16, f32[3,34,34,256]{3,1,0,2:T(8,128)S(1)} %fusion.28, f32[3,34,34,256]{3,1,0,2:T(8,128)} %fusion.25, ...), kind=kOutput, calls=%fused_computation.249 | convolution fusion | flops 462547968 | bytes 36067328 | tf_op jit(solution)/shard_map/dot_general | solution.py:111
  200.9 4.4 %all-to-all-start.2 = ((bf16[8,1,3,4,32,256]{5,4,3,2,1,0:T(8,128)(2,1)}), bf16[8,1,3,4,32,256]{5,4,3,2,1,0:T(8,128)(2,1)}, u32[]{:S(2)}, u32[]{:S(2)}) async-start(bf16[8,1,3,4,32,256]{5,4,3,2,1,0:T(8,128)(2,1)} %broadcast_in_dim.78), calls=%async_computation.2 | async-start | bytes 3145728 | tf_op jit(solution)/shard_map/all_to_all | solution.py:11
  205.3 3.3 convert_add_fusion
  208.7 2.2 slice.427
  216.7 9.7 %all-to-all-done.2 = bf16[8,1,3,4,32,256]{5,4,3,2,1,0:T(8,128)(2,1)} async-done(((bf16[8,1,3,4,32,256]{5,4,3,2,1,0:T(8,128)(2,1)}), bf16[8,1,3,4,32,256]{5,4,3,2,1,0:T(8,128)(2,1)}, u32[]{:S(2)}, u32[]{:S(2)}) %all-to-all-start.2) | async-done | bytes 1572896 | tf_op jit(solution)/shard_map/all_to_all | solution.py:11
  226.4 2.0 gather_fusion.2
  250.1 152.0 %all-reduce.6.cloned.1.call-done = (f32[3,3,256,256]{3,2,1,0:T(8,128)}, f32[3,3,256,256]{3,2,1,0:T(8,128)}) async-done(((f32[3,3,256,256]{3,2,1,0:T(8,128)}, f32[3,3,256,256]{3,2,1,0:T(8,128)}), (f32[3,3,256,256]{3,2,1,0:T(8,128)}, f32[3,3,256,256]{3,2,1,0:T(8,128)})) %all-reduce.6.cloned.1.call-update) | async-done | bytes 4718608
  403.7 4.0 all-to-all-start.4
  408.6 5.9 %all-to-all-done.4 = f32[8,3,3,2,256]{4,3,2,1,0:T(2,128)S(1)} async-done(((f32[8,3,3,2,256]{4,3,2,1,0:T(2,128)}), f32[8,3,3,2,256]{4,3,2,1,0:T(2,128)S(1)}, u32[]{:S(2)}, u32[]{:S(2)}) %all-to-all-start.4) | async-done | bytes 147488 | tf_op jit(solution)/shard_map/all_to_all | solution.py:11
  415.2 3.4 all-to-all-start.3
  418.6 2.0 copy.414
  420.8 4.5 %all-to-all-done.3 = f32[8,3,3,2,256]{4,3,2,1,0:T(2,128)S(1)} async-done(((f32[8,3,3,2,256]{4,3,2,1,0:T(2,128)}), f32[8,3,3,2,256]{4,3,2,1,0:T(2,128)S(1)}, u32[]{:S(2)}, u32[]{:S(2)}) %all-to-all-start.3) | async-done | bytes 147488 | tf_op jit(solution)/shard_map/all_to_all | solution.py:11
  (174 shorter events, 55.3 us)
Async XLA Ops:
  7.2 55.4 %all-gather.2.cloned.1.call-start = ((), (), s32[]{:S(2)}) async-start(), calls=%async_computation.5 | async-start | bytes 2506752 | tf_op jit(solution)/shard_map/all_gather | solution.py:159
  7.9 2.4 copy-start
  11.8 5.6 %copy-start.40 = (s32[3,4,3]{2,1,0:T(4,128)S(1)}, s32[3,4,3]{2,1,0:T(4,128)}, u32[]{:S(2)}) copy-start(s32[3,4,3]{2,1,0:T(4,128)} %param.7) | copy-start | bytes 436
  11.8 28.5 %all-to-all-start = ((bf16[8,1,3,4,32,256]{5,4,3,2,1,0:T(8,128)(2,1)}), bf16[8,1,3,4,32,256]{5,4,3,2,1,0:T(8,128)(2,1)S(1)}, u32[]{:S(2)}, u32[]{:S(2)}) async-start(bf16[8,1,3,4,32,256]{5,4,3,2,1,0:T(8,128)(2,1)} %broadcast_in_dim.38), calls=%async_computation | async-start | bytes 3145728 | tf_op jit(solution)/shard_map/all_to_all | solution.py:11
  44.6 28.3 %copy-start.7 = (bf16[3,32,32,256]{3,2,1,0:T(8,128)(2,1)}, bf16[3,32,32,256]{3,2,1,0:T(8,128)(2,1)S(1)}, u32[]{:S(2)}) copy-start(bf16[3,32,32,256]{3,2,1,0:T(8,128)(2,1)S(1)} %get-tuple-element.46) | copy-start | bytes 4718596
  47.0 1.3 copy-start.3
  47.1 2.0 copy-start.5
  62.6 2.9 copy-start.22
  65.5 14.8 %copy-start.26 = (bf16[3,3,256,256]{3,2,1,0:T(8,128)(2,1)}, bf16[3,3,256,256]{3,2,1,0:T(8,128)(2,1)S(1)}, u32[]{:S(2)}) copy-start(bf16[3,3,256,256]{3,2,1,0:T(8,128)(2,1)S(1)} %get-tuple-element.18) | copy-start | bytes 3538948
  65.5 1.8 copy-start.21
  67.4 1.8 copy-start.9
  72.9 1.9 copy-start.20
  74.8 1.8 copy-start.19
  76.6 3.7 copy-start.18
  95.3 4.9 %copy-start.14 = (bf16[3,3,256,256]{3,2,1,0:T(8,128)(2,1)S(1)}, bf16[3,3,256,256]{3,2,1,0:T(8,128)(2,1)}, u32[]{:S(2)}) copy-start(bf16[3,3,256,256]{3,2,1,0:T(8,128)(2,1)} %get-tuple-element.19) | copy-start | bytes 3538948
  95.4 26.9 %all-to-all-start.1 = ((bf16[8,1,3,4,32,256]{5,4,3,2,1,0:T(8,128)(2,1)}), bf16[8,1,3,4,32,256]{5,4,3,2,1,0:T(8,128)(2,1)}, u32[]{:S(2)}, u32[]{:S(2)}) async-start(bf16[8,1,3,4,32,256]{5,4,3,2,1,0:T(8,128)(2,1)} %broadcast_in_dim.75), calls=%async_computation.1 | async-start | bytes 3145728 | tf_op jit(solution)/shard_map/all_to_all | solution.py:11
  127.7 10.9 %copy-start.25 = (bf16[3,32,32,256]{3,1,0,2:T(8,128)(2,1)}, bf16[3,32,32,256]{3,1,0,2:T(8,128)(2,1)S(1)}, u32[]{:S(2)}) copy-start(bf16[3,32,32,256]{3,1,0,2:T(8,128)(2,1)S(1)} %get-tuple-element.41) | copy-start | bytes 4718596
  127.7 13.1 %copy-start.23 = (bf16[3,32,32,256]{3,1,0,2:T(8,128)(2,1)}, bf16[3,32,32,256]{3,1,0,2:T(8,128)(2,1)S(1)}, u32[]{:S(2)}) copy-start(bf16[3,32,32,256]{3,1,0,2:T(8,128)(2,1)S(1)} %get-tuple-element.40) | copy-start | bytes 4718596
  140.8 2.8 copy-start.12
  155.4 1.4 copy-start.24
  158.1 2.4 copy-start.15
  180.7 13.1 %copy-start.31 = (bf16[3,32,32,256]{3,1,0,2:T(8,128)(2,1)S(1)}, bf16[3,32,32,256]{3,1,0,2:T(8,128)(2,1)}, u32[]{:S(2)}) copy-start(bf16[3,32,32,256]{3,1,0,2:T(8,128)(2,1)} %get-tuple-element.28) | copy-start | bytes 4718596
  193.8 1.4 copy-start.30
  195.2 1.4 copy-start.29
  196.6 1.4 copy-start.32
  200.9 4.5 %copy-start.17 = (bf16[1,3,32,32,256]{4,3,2,1,0:T(8,128)(2,1)S(1)}, bf16[1,3,32,32,256]{4,3,2,1,0:T(8,128)(2,1)}, u32[]{:S(2)}) copy-start(bf16[1,3,32,32,256]{4,3,2,1,0:T(8,128)(2,1)} %param.6) | copy-start | bytes 4718596
  200.9 25.6 %all-to-all-start.2 = ((bf16[8,1,3,4,32,256]{5,4,3,2,1,0:T(8,128)(2,1)}), bf16[8,1,3,4,32,256]{5,4,3,2,1,0:T(8,128)(2,1)}, u32[]{:S(2)}, u32[]{:S(2)}) async-start(bf16[8,1,3,4,32,256]{5,4,3,2,1,0:T(8,128)(2,1)} %broadcast_in_dim.78), calls=%async_computation.2 | async-start | bytes 3145728 | tf_op jit(solution)/shard_map/all_to_all | solution.py:11
  205.3 196.8 %all-reduce.6.cloned.1.call-start = ((), (), s32[]{:S(2)}) async-start(), calls=%async_computation.6 | async-start | bytes 9437184
  208.6 2.7 copy-start.11
  208.6 2.7 copy-start.37
  208.6 2.7 copy-start.38
  208.6 2.6 copy-start.39
  208.6 2.7 copy-start.33
  208.7 2.7 copy-start.34
  208.7 2.7 copy-start.35
  211.3 1.4 copy-start.28
  212.7 1.4 copy-start.27
  214.1 0.9 copy-start.36
  215.1 16.8 %copy-start.2 = (f32[1,3,30,32,256]{4,2,1,3,0:T(8,128)S(1)}, f32[1,3,30,32,256]{4,2,1,3,0:T(8,128)}, u32[]{:S(2)}) copy-start(f32[1,3,30,32,256]{4,2,1,3,0:T(8,128)} %slice.427) | copy-start | bytes 8847364
  232.6 1.9 copy-start.13
  234.5 1.6 copy-start.6
  238.7 1.4 copy-start.10
  240.1 1.4 copy-start.1
  241.5 1.4 copy-start.8
  242.9 1.6 copy-start.4
  250.1 168.5 %copy-start.16 = (bf16[1,3,32,32,256]{4,2,1,3,0:T(8,128)(2,1)S(1)}, bf16[1,3,32,32,256]{4,2,1,3,0:T(8,128)(2,1)}, u32[]{:S(2)}) copy-start(bf16[1,3,32,32,256]{4,2,1,3,0:T(8,128)(2,1)} %get-tuple-element.17) | copy-start | bytes 4718596
  403.7 10.8 %all-to-all-start.4 = ((f32[8,3,3,2,256]{4,3,2,1,0:T(2,128)}), f32[8,3,3,2,256]{4,3,2,1,0:T(2,128)S(1)}, u32[]{:S(2)}, u32[]{:S(2)}) async-start(f32[8,3,3,2,256]{4,3,2,1,0:T(2,128)} %broadcast_in_dim.80), calls=%async_computation.4 | async-start | bytes 294912 | tf_op jit(solution)/shard_map/all_to_all | solution.py:11
  415.2 10.1 %all-to-all-start.3 = ((f32[8,3,3,2,256]{4,3,2,1,0:T(2,128)}), f32[8,3,3,2,256]{4,3,2,1,0:T(2,128)S(1)}, u32[]{:S(2)}, u32[]{:S(2)}) async-start(f32[8,3,3,2,256]{4,3,2,1,0:T(2,128)} %broadcast_in_dim.79), calls=%async_computation.3 | async-start | bytes 294912 | tf_op jit(solution)/shard_map/all_to_all | solution.py:11
Sparse Core Ops, SparseCore 0:
  10.2 52.3 all-gather.1
  250.2 151.8 all-reduce.5
where the time goes:
time: 439 us; the launch traced here: 433 us
  waiting for transfers between devices  224 us (51%)
  matrix products  109 us (25%)
  local copies, waits for them, and re-layouts  43.6 us (10%)
  starting transfers between devices  22.4 us (5%)
  other arithmetic  20 us (5%)
  between operations  15.1 us (3%)
    unnamed x3, waiting for transfers between devices  153 us
    all_to_all x5, waiting for transfers between devices, copy_for_each(): lax.all_to_all(jnp.broadcast_to(value[None], (count, *value.shape)), axis...  62.2 us
    dot_general x18, matrix products, convolve(): jnp.dot(patches, kernel[row_off, col_off], preferred_element_type=jnp.flo...  52.3 us
    dot_general x9, matrix products, input_grad(): lax.dot_general(window, kernel[row_off, col_off], (((1,), (1,)), ((), ())...  33.1 us
    dot_general x18, matrix products, weight_grad(): lax.dot_general(patches, flat_grad, (((0,), (0,)), ((), ())), preferred_e...  23.2 us
    all_to_all x5, starting transfers between devices, copy_for_each(): lax.all_to_all(jnp.broadcast_to(value[None], (count, *value.shape)), axis...  22.3 us
    unnamed x91, local copies, waits for them, and re-layouts  14.6 us
    dot_general x3, local copies, waits for them, and re-layouts, convolve(): jnp.dot(patches, kernel[row_off, col_off], preferred_element_type=jnp.flo...  11 us
  transfers between devices with their start and end apart: 7, of which 7 were waited for; matrix products, arithmetic and copies ran while one was open for 7% of the time, Pallas kernels for 0%

commit v1 on v0

v1 whole, which is shorter than its diff:
```python
import jax
import jax.numpy as jnp
from jax import lax
from jax.experimental import pallas as pl
from jax.experimental.pallas import tpu as pltpu
from jax.sharding import PartitionSpec as P

BF = jnp.bfloat16
F32 = jnp.float32
TILES, SIDE, CH = 3, 32, 256
CELLS = SIDE * SIDE
SLOTS = 7
GOT, BACK = 64, 76


def vmem():
    return pl.BlockSpec(memory_space=pltpu.VMEM)


def smem():
    return pl.BlockSpec(memory_space=pltpu.SMEM)


def whole(shape):
    zeros = (0,) * len(shape)
    return pl.BlockSpec(shape, lambda t: zeros)


def per_tile(*tail):
    zeros = (0,) * (len(tail) - 1)
    return pl.BlockSpec(tail, lambda t: (t, *zeros))


def struct(shape, dtype):
    return jax.ShapeDtypeStruct(shape, dtype)


def params(steps=0):
    if steps:
        return pltpu.CompilerParams(
            dimension_semantics=("arbitrary",), vmem_limit_bytes=60 * 1024 * 1024
        )
    return pltpu.CompilerParams(vmem_limit_bytes=60 * 1024 * 1024)


def cost(flops, moved):
    return pl.CostEstimate(flops=flops, bytes_accessed=moved, transcendentals=0)


def take(halves, rows):
    return jnp.concatenate([halves[0, rows, :], halves[1, rows, :]], axis=1)


def put(halves, rows, value):
    halves[0, rows, :] = value[:, 0:128]
    halves[1, rows, :] = value[:, 128:256]


def fill(routes_ref, strips, send_ref):
    for slot in range(send_ref.shape[0]):
        send_ref[slot] = strips[routes_ref[slot]]


def pack_kernel(me_ref, adj_ref, field_ref, send_ref, routes_ref, column, strips):
    peers = adj_ref.shape[0]
    me = me_ref[0]
    for slot in range(GOT):
        routes_ref[slot] = 0
    for peer in range(peers):
        sent = jnp.int32(0)
        for edge in range(4 * TILES):
            other = adj_ref[peer, edge * 3]
            owner = lax.div(other, TILES)
            mine = (owner == me).astype(jnp.int32)
            slot = peer * SLOTS + jnp.minimum(sent, SLOTS - 1)
            strip = (other - owner * TILES) * 4 + adj_ref[peer, edge * 3 + 1]
            routes_ref[jnp.where(owner == me, slot, GOT - 1)] = jnp.where(owner == me, strip, 0)
            sent += mine
    owners = []
    for edge in range(4 * TILES):
        owners.append(lax.div(adj_ref[me, edge * 3], TILES))
        before = jnp.int32(0)
        for there in range(edge):
            before += (owners[there] == owners[edge]).astype(jnp.int32)
        routes_ref[GOT + edge] = owners[edge] * SLOTS + jnp.minimum(before, SLOTS - 1)
        routes_ref[BACK + edge] = adj_ref[me, edge * 3 + 2]
    for tile in range(TILES):
        strips[tile * 4] = field_ref[tile, 0]
        strips[tile * 4 + 1] = field_ref[tile, SIDE - 1]
        for edge, first, lane in ((2, 0, 0), (3, SIDE - 8, 7)):
            near = field_ref[tile, :, first : first + 8].astype(F32).reshape(SIDE * 8, CH)
            put(column, slice(None), near)
            strips[tile * 4 + edge] = take(column, pl.ds(lane, SIDE, stride=8)).astype(BF)
    fill(routes_ref, strips, send_ref)


def pack(me, adjacency, field):
    peers = adjacency.shape[0]
    return pl.pallas_call(
        pack_kernel,
        name="pack",
        out_shape=(struct((peers * SLOTS, SIDE, CH), BF), struct((BACK + 12,), jnp.int32)),
        in_specs=[smem(), smem(), vmem()],
        out_specs=(vmem(), smem()),
        scratch_shapes=[
            pltpu.VMEM((2, SIDE * 8, 128), F32),
            pltpu.VMEM((4 * TILES, SIDE, CH), BF),
        ],
        compiler_params=params(),
        cost_estimate=cost(0, 3_000_000),
    )(me, adjacency, field)


def pick(rows, shift_of_block, backwards):
    row = lax.broadcasted_iota(jnp.int32, (rows, SIDE), 0)
    cell = lax.broadcasted_iota(jnp.int32, (rows, SIDE), 1)
    block = row // SIDE
    place = row - block * SIDE
    source = place + shift_of_block(block)
    inside = (source >= 0) & (source < SIDE)
    if backwards is not None:
        source = jnp.where(backwards == 1, SIDE - 1 - source, source)
    return jnp.where(inside & (cell == source), 1.0, 0.0).astype(BF)


def dot(left, right):
    return jnp.dot(left, right, preferred_element_type=F32)


def dot_rows(left, right):
    return lax.dot_general(left, right, (((0,), (0,)), ((), ())), preferred_element_type=F32)


def block_of_edge(edge, k):
    return (k, 6 + k, 3 * k, 3 * k + 2)[edge]


EDGE_ROWS = (
    pl.ds(0, SIDE),
    pl.ds(CELLS - SIDE, SIDE),
    pl.ds(0, SIDE, stride=SIDE),
    pl.ds(SIDE - 1, SIDE, stride=SIDE),
)


def spread(source, out_ref, ascending):
    first = lax.broadcasted_iota(jnp.int32, (SIDE, CH), 0) == 0
    last = lax.broadcasted_iota(jnp.int32, (SIDE, CH), 0) == SIDE - 1

    def one(i, carry):
        row = source(i).astype(F32)
        earlier = jnp.where(first, 0.0, pltpu.roll(row, 1, 0)).astype(BF)
        later = jnp.where(last, 0.0, pltpu.roll(row, SIDE - 1, 0)).astype(BF)
        at = pl.ds(pl.multiple_of((i + 1) * SIDE, SIDE), SIDE)
        low, high = (earlier, later) if ascending else (later, earlier)
        out_ref[at, 0:CH] = low
        out_ref[at, CH : 2 * CH] = row.astype(BF)
        out_ref[at, 2 * CH : 3 * CH] = high
        return carry

    lax.fori_loop(0, SIDE, one, 0, unroll=4)


def clear_margin(out_ref):
    zero = jnp.zeros((SIDE, 3 * CH), BF)
    out_ref[0:SIDE, :] = zero
    out_ref[CELLS + SIDE : CELLS + 2 * SIDE, :] = zero


def conv_kernel(turned, shards, core_ref, field_ref, mine_ref, theirs_ref, *refs):
    if turned:
        part_ref, kernel_ref, turned_ref, wide = refs
    else:
        part_ref, kernel_ref, wide = refs
    depth = CH // shards
    core = core_ref[0]

    @pl.when(pl.program_id(0) == 0)
    def _():
        clear_margin(wide)
        for pair in range(shards // 2):
            for source, side in ((mine_ref, core), (theirs_ref, 1 - core)):
                for tap in range(9):
                    at = pl.multiple_of(tap * CH + pair * 2 * depth + side * depth, depth)
                    kernel_ref[pl.ds(at, depth), :] = source[pair, 0, tap]
        if turned:
            for tap in range(9):
                turned_ref[tap * CH : (tap + 1) * CH, :] = kernel_ref[tap * CH : (tap + 1) * CH, :].T

    spread(lambda i: field_ref[0, i], wide, True)

    def chunk(c, carry):
        total = None
        for p in range(3):
            at = pl.multiple_of(c * CH + p * SIDE, SIDE)
            term = dot(wide[pl.ds(at, CH), :], kernel_ref[p * 3 * CH : (p + 1) * 3 * CH, :])
            total = term if total is None else total + term
        part_ref[pl.ds(pl.multiple_of(c * CH, CH), CH), :] = total
        return carry

    lax.fori_loop(0, CELLS // CH, chunk, 0)


def conv(core, field, mine, theirs, layer, turned):
    pieces = pl.BlockSpec((mine.shape[0], 1, *mine.shape[2:]), lambda t: (0, layer, 0, 0, 0))
    shards = mine.shape[0] * 2
    outs = [struct((TILES * CELLS, CH), F32), struct((9 * CH, CH), BF)]
    specs = [per_tile(CELLS, CH), whole((9 * CH, CH))]
    if turned:
        outs.append(struct((9 * CH, CH), BF))
        specs.append(whole((9 * CH, CH)))
    return pl.pallas_call(
        lambda *refs: conv_kernel(turned, shards, *refs),
        name="conv_turned" if turned else "conv",
        out_shape=tuple(outs),
        grid=(TILES,),
        in_specs=[smem(), per_tile(1, SIDE, SIDE, CH), pieces, pieces],
        out_specs=tuple(specs),
        scratch_shapes=[pltpu.VMEM((CELLS + 2 * SIDE, 3 * CH), BF)],
        compiler_params=params(1),
        cost_estimate=cost(3_600_000_000, 7_000_000),
    )(core, field, mine, theirs)


def add_rims(routes_ref, got_ref, kernel_ref, rows3, rim_part):
    for edge in range(4):
        for tile in range(TILES):
            back = routes_ref[BACK + tile * 4 + edge]
            choose = pick(3 * SIDE, lambda block: block - 1, back)
            shifted = dot(choose, got_ref[routes_ref[GOT + tile * 4 + edge]]).astype(BF)
            for k in range(3):
                rows3[tile * SIDE : (tile + 1) * SIDE, k * CH : (k + 1) * CH] = shifted[
                    k * SIDE : (k + 1) * SIDE
                ]
        total = None
        for k in range(3):
            block = block_of_edge(edge, k)
            term = dot(
                rows3[:, k * CH : (k + 1) * CH], kernel_ref[block * CH : (block + 1) * CH, :]
            )
            total = term if total is None else total + term
        rim_part[edge] = total


def with_rims(part_ref, rim_part, out):
    tile = pl.program_id(0)
    put(out, slice(None), part_ref[...])
    for edge in range(4):
        rows = EDGE_ROWS[edge]
        add = rim_part[edge, pl.ds(pl.multiple_of(tile * SIDE, SIDE), SIDE), :]
        put(out, rows, take(out, rows) + add)


def finish_kernel(
    routes_ref,
    part_ref,
    field_ref,
    got_ref,
    kernel_ref,
    state_ref,
    slope_ref,
    send_ref,
    rows3,
    rim_part,
    fresh,
    strips,
):
    tile = pl.program_id(0)

    @pl.when(tile == 0)
    def _():
        add_rims(routes_ref, got_ref, kernel_ref, rows3, rim_part)

    with_rims(part_ref, rim_part, fresh)

    def one(i, carry):
        at = pl.ds(pl.multiple_of(i * SIDE, SIDE), SIDE)
        v = take(fresh, at)
        s = 1.0 / (1.0 + jnp.exp(-v))
        updated = field_ref[0, i].astype(F32) + v * s
        put(fresh, at, updated)
        state_ref[0, i] = updated.astype(BF)
        slope_ref[at, :] = s * (1.0 + v * (1.0 - s))
        return carry

    lax.fori_loop(0, SIDE, one, 0, unroll=4)
    for edge in range(4):
        strips[tile * 4 + edge] = take(fresh, EDGE_ROWS[edge]).astype(BF)

    @pl.when(tile == TILES - 1)
    def _():
        fill(routes_ref, strips, send_ref)


def finish(routes, part, field, got, kernel):
    return pl.pallas_call(
        finish_kernel,
        name="finish",
        out_shape=(
            struct(field.shape, BF),
            struct(part.shape, F32),
            struct(got.shape, BF),
        ),
        grid=(TILES,),
        in_specs=[
            smem(),
            per_tile(CELLS, CH),
            per_tile(1, SIDE, SIDE, CH),
            whole(got.shape),
            whole(kernel.shape),
        ],
        out_specs=(per_tile(1, SIDE, SIDE, CH), per_tile(CELLS, CH), whole(got.shape)),
        scratch_shapes=[
            pltpu.VMEM((TILES * SIDE, 3 * CH), BF),
            pltpu.VMEM((4, TILES * SIDE, CH), F32),
            pltpu.VMEM((2, CELLS, 128), F32),
            pltpu.VMEM((4 * TILES, SIDE, CH), BF),
        ],
        compiler_params=params(1),
        cost_estimate=cost(200_000_000, 10_000_000),
    )(routes, part, field, got, kernel)


def note_strips(grad, triples, tile):
    choose = pick(3 * SIDE, lambda block: 1 - block, None)
    for edge in range(4):
        shifted = dot(choose, take(grad, EDGE_ROWS[edge]).astype(BF)).astype(BF)
        for k in range(3):
            triples[
                edge, pl.ds(pl.multiple_of(tile * SIDE, SIDE), SIDE), k * CH : (k + 1) * CH
            ] = shifted[k * SIDE : (k + 1) * SIDE]


def last_kernel(
    routes_ref,
    part_ref,
    field_ref,
    got_ref,
    kernel_ref,
    turned_ref,
    cot_ref,
    state_ref,
    grad_ref,
    send_ref,
    triples_ref,
    rows3,
    rim_part,
    fresh,
    strips,
):
    tile = pl.program_id(0)

    @pl.when(tile == 0)
    def _():
        add_rims(routes_ref, got_ref, kernel_ref, rows3, rim_part)

    with_rims(part_ref, rim_part, fresh)

    def one(i, carry):
        at = pl.ds(pl.multiple_of(i * SIDE, SIDE), SIDE)
        v = take(fresh, at)
        s = 1.0 / (1.0 + jnp.exp(-v))
        state_ref[0, i] = (field_ref[0, i].astype(F32) + v * s).astype(BF)
        grad = cot_ref[0, i].astype(F32) * s * (1.0 + v * (1.0 - s))
        put(fresh, at, grad)
        grad_ref[at, :] = grad.astype(BF)
        return carry

    lax.fori_loop(0, SIDE, one, 0, unroll=4)
    note_strips(fresh, triples_ref, tile)

    @pl.when(tile == TILES - 1)
    def _():
        for edge in range(4):
            total = None
            for k in range(3):
                block = block_of_edge(edge, k)
                term = dot(
                    triples_ref[edge, :, k * CH : (k + 1) * CH],
                    turned_ref[block * CH : (block + 1) * CH, :],
                )
                total = term if total is None else total + term
            for there in range(TILES):
                strips[there * 4 + edge] = total[there * SIDE : (there + 1) * SIDE].astype(BF)
        fill(routes_ref, strips, send_ref)


def last(routes, part, field, got, kernel, turned, cotangent):
    triples = (4, TILES * SIDE, 3 * CH)
    return pl.pallas_call(
        last_kernel,
        name="last",
        out_shape=(
            struct(field.shape, BF),
            struct((TILES * CELLS, CH), BF),
            struct(got.shape, BF),
            struct(triples, BF),
        ),
        grid=(TILES,),
        in_specs=[
            smem(),
            per_tile(CELLS, CH),
            per_tile(1, SIDE, SIDE, CH),
            whole(got.shape),
            whole(kernel.shape),
            whole(turned.shape),
            per_tile(1, SIDE, SIDE, CH),
        ],
        out_specs=(
            per_tile(1, SIDE, SIDE, CH),
            per_tile(CELLS, CH),
            whole(got.shape),
            whole(triples),
        ),
        scratch_shapes=[
            pltpu.VMEM((TILES * SIDE, 3 * CH), BF),
            pltpu.VMEM((4, TILES * SIDE, CH), F32),
            pltpu.VMEM((2, CELLS, 128), F32),
            pltpu.VMEM((4 * TILES, SIDE, CH), BF),
        ],
        compiler_params=params(1),
        cost_estimate=cost(400_000_000, 12_000_000),
    )(routes, part, field, got, kernel, turned, cotangent)


def outer(field, wide, across, total):
    across[...] = field.reshape(CELLS, CH).T

    def one(p, carry):
        at = pl.multiple_of((2 - p) * SIDE, SIDE)
        total[p] = total[p] + dot(across[...], wide[pl.ds(at, CELLS), :])
        return carry

    lax.fori_loop(0, 3, one, 0)


def outer_rims(routes_ref, got_ref, triples, total, flat):
    for edge in range(4):
        for tile in range(TILES):
            back = routes_ref[BACK + tile * 4 + edge]
            choose = pick(SIDE, lambda block: 0, back)
            flat[tile * SIDE : (tile + 1) * SIDE, :] = dot(
                choose, got_ref[routes_ref[GOT + tile * 4 + edge]]
            ).astype(BF)
        for k in range(3):
            p, q = divmod(block_of_edge(edge, k), 3)
            lanes = slice(q * CH, (q + 1) * CH)
            total[p, :, lanes] = total[p, :, lanes] + dot_rows(
                flat[...], triples[edge, :, k * CH : (k + 1) * CH]
            )


def hand_over(core, total, kept_ref, given_ref):
    pairs = kept_ref.shape[0]
    depth = kept_ref.shape[2]
    for pair in range(pairs):
        own = pl.ds(pl.multiple_of(pair * 2 * depth + core * depth, depth), depth)
        other = pl.ds(pl.multiple_of(pair * 2 * depth + (1 - core) * depth, depth), depth)
        for tap in range(9):
            p, q = divmod(tap, 3)
            kept_ref[pair, tap] = total[p, own, q * CH : (q + 1) * CH]
            given_ref[pair, tap] = total[p, other, q * CH : (q + 1) * CH].astype(BF)


def second_kernel(
    routes_ref,
    core_ref,
    field_ref,
    grad_ref,
    got_ref,
    triples_ref,
    turned_ref,
    back_ref,
    kept_ref,
    given_ref,
    wide,
    across,
    total,
    flat,
):
    tile = pl.program_id(0)

    @pl.when(tile == 0)
    def _():
        clear_margin(wide)
        total[...] = jnp.zeros_like(total)

    spread(lambda i: grad_ref[pl.ds(pl.multiple_of(i * SIDE, SIDE), SIDE), :], wide, False)

    def chunk(c, carry):
        result = None
        for p in range(3):
            at = pl.multiple_of(c * CH + (2 - p) * SIDE, SIDE)
            term = dot(wide[pl.ds(at, CH), :], turned_ref[p * 3 * CH : (p + 1) * 3 * CH, :])
            result = term if result is None else result + term
        back_ref[pl.ds(pl.multiple_of(c * CH, CH), CH), :] = result
        return carry

    lax.fori_loop(0, CELLS // CH, chunk, 0)
    outer(field_ref[0], wide, across, total)

    @pl.when(tile == TILES - 1)
    def _():
        outer_rims(routes_ref, got_ref, triples_ref, total, flat)
        hand_over(core_ref[0], total, kept_ref, given_ref)


def second(routes, core, field, grad, got, triples, turned, pairs, depth):
    half = (pairs, 9, depth, CH)
    return pl.pallas_call(
        second_kernel,
        name="second",
        out_shape=(struct((TILES * CELLS, CH), F32), struct(half, F32), struct(half, BF)),
        grid=(TILES,),
        in_specs=[
            smem(),
            smem(),
            per_tile(1, SIDE, SIDE, CH),
            per_tile(CELLS, CH),
            whole(got.shape),
            whole(triples.shape),
            whole(turned.shape),
        ],
        out_specs=(per_tile(CELLS, CH), whole(half), whole(half)),
        scratch_shapes=[
            pltpu.VMEM((CELLS + 2 * SIDE, 3 * CH), BF),
            pltpu.VMEM((CH, CELLS), BF),
            pltpu.VMEM((3, CH, 3 * CH), F32),
            pltpu.VMEM((TILES * SIDE, CH), BF),
        ],
        compiler_params=params(1),
        cost_estimate=cost(7_200_000_000, 12_000_000),
    )(routes, core, field, grad, got, triples, turned)


def first_kernel(
    routes_ref,
    core_ref,
    field_ref,
    cot_ref,
    back_ref,
    slope_ref,
    got_ref,
    returned_ref,
    kept_ref,
    given_ref,
    wide,
    across,
    total,
    flat,
    fresh,
    triples,
):
    tile = pl.program_id(0)

    @pl.when(tile == 0)
    def _():
        clear_margin(wide)
        total[...] = jnp.zeros_like(total)

    def one(i, carry):
        at = pl.ds(pl.multiple_of(i * SIDE, SIDE), SIDE)
        put(fresh, at, cot_ref[0, i].astype(F32) + back_ref[at, :])
        return carry

    lax.fori_loop(0, SIDE, one, 0, unroll=4)
    for edge in range(4):
        back = routes_ref[BACK + tile * 4 + edge]
        choose = pick(SIDE, lambda block: 0, back)
        rows = EDGE_ROWS[edge]
        add = dot(choose, returned_ref[routes_ref[GOT + tile * 4 + edge]])
        put(fresh, rows, take(fresh, rows) + add)

    def two(i, carry):
        at = pl.ds(pl.multiple_of(i * SIDE, SIDE), SIDE)
        put(fresh, at, take(fresh, at) * slope_ref[at, :])
        return carry

    lax.fori_loop(0, SIDE, two, 0, unroll=4)
    note_strips(fresh, triples, tile)
    spread(lambda i: take(fresh, pl.ds(pl.multiple_of(i * SIDE, SIDE), SIDE)), wide, False)
    outer(field_ref[0], wide, across, total)

    @pl.when(tile == TILES - 1)
    def _():
        outer_rims(routes_ref, got_ref, triples, total, flat)
        hand_over(core_ref[0], total, kept_ref, given_ref)


def first(routes, core, field, cotangent, back, slope, got, returned, pairs, depth):
    half = (pairs, 9, depth, CH)
    return pl.pallas_call(
        first_kernel,
        name="first",
        out_shape=(struct(half, F32), struct(half, BF)),
        grid=(TILES,),
        in_specs=[
            smem(),
            smem(),
            per_tile(1, SIDE, SIDE, CH),
            per_tile(1, SIDE, SIDE, CH),
            per_tile(CELLS, CH),
            per_tile(CELLS, CH),
            whole(got.shape),
            whole(returned.shape),
        ],
        out_specs=(whole(half), whole(half)),
        scratch_shapes=[
            pltpu.VMEM((CELLS + 2 * SIDE, 3 * CH), BF),
            pltpu.VMEM((CH, CELLS), BF),
            pltpu.VMEM((3, CH, 3 * CH), F32),
            pltpu.VMEM((TILES * SIDE, CH), BF),
            pltpu.VMEM((2, CELLS, 128), F32),
            pltpu.VMEM((4, TILES * SIDE, 3 * CH), BF),
        ],
        compiler_params=params(1),
        cost_estimate=cost(3_600_000_000, 12_000_000),
    )(routes, core, field, cotangent, back, slope, got, returned)


def cut_kernel(kept_ref, got_ref, out_ref, rows):
    pairs, _, depth, _ = kept_ref.shape
    run = 9 * depth // 4
    for pair in range(pairs):
        for tap in range(9):
            rows[tap * depth : (tap + 1) * depth, :] = kept_ref[pair, tap] + got_ref[
                pair, tap
            ].astype(F32)
        for peer in range(8):
            high, low = divmod(peer, 4)
            out_ref[pair * 8 + peer] = rows[
                low * run : (low + 1) * run, high * 128 : (high + 1) * 128
            ].astype(BF)


def cut(kept, got):
    pairs, _, depth, _ = kept.shape
    return pl.pallas_call(
        cut_kernel,
        name="cut",
        out_shape=struct((pairs * 8, 9 * depth // 4, 128), BF),
        in_specs=[vmem(), vmem()],
        out_specs=vmem(),
        scratch_shapes=[pltpu.VMEM((9 * depth, CH), F32)],
        compiler_params=params(),
        cost_estimate=cost(0, 3_000_000),
    )(kept, got)


def sum_kernel(*refs):
    *in_refs, out_ref = refs
    for layer, source in enumerate(in_refs):
        summed = source[0].astype(F32)
        for other in range(1, source.shape[0]):
            summed = summed + source[other].astype(F32)
        for peer in range(out_ref.shape[0]):
            run = summed.shape[0]
            out_ref[peer, layer * run : (layer + 1) * run] = summed


def sum_all(parts, peers):
    return pl.pallas_call(
        sum_kernel,
        name="sum_all",
        out_shape=struct((peers, len(parts) * parts[0].shape[1], 128), F32),
        in_specs=[vmem()] * len(parts),
        out_specs=vmem(),
        compiler_params=params(),
        cost_estimate=cost(0, 2_000_000),
    )(*parts)


def join_kernel(in_ref, out_ref):
    peers = in_ref.shape[0]
    run = in_ref.shape[1] // 2
    rows_all = out_ref.shape[0] // 2
    for layer in range(2):
        for peer in range(peers):
            high, low = divmod(peer, 4)
            at = layer * rows_all + low * run
            out_ref[at : at + run, high * 128 : (high + 1) * 128] = in_ref[
                peer, layer * run : (layer + 1) * run
            ]


def join(blocks, depth):
    return pl.pallas_call(
        join_kernel,
        name="join",
        out_shape=struct((2 * 9 * depth, CH), F32),
        in_specs=[vmem()],
        out_specs=vmem(),
        compiler_params=params(),
        cost_estimate=cost(0, 600_000),
    )(blocks)


def exchange(value, axes, groups=None):
    return lax.all_to_all(value, axes, 0, 0, tiled=True, axis_index_groups=groups)


def solution(mesh):
    shards, peers = mesh.shape["dp"], mesh.shape["space"]
    pairs, depth = shards // 2, CH // shards
    same_core = [[pair * 2 + core for pair in range(pairs)] for core in range(2)]
    same_core_all = [
        [(pair * 2 + core) * peers + peer for pair in range(pairs) for peer in range(peers)]
        for core in range(2)
    ]
    swap = [(index, index ^ 1) for index in range(shards)]

    def gather(shard):
        mine = exchange(
            jnp.broadcast_to(shard[None], (pairs, *shard.shape)), "dp", same_core
        )
        return mine, lax.ppermute(mine, "dp", swap)

    def trade(strips):
        return exchange(strips.reshape(peers, SLOTS, SIDE, CH), "space").reshape(strips.shape)

    def halve(kept, given):
        return cut(kept, lax.ppermute(given, "dp", swap))

    def per_device(inputs, kernels, cotangent, adjacency):
        field = inputs[0]
        cot = cotangent[0]
        core = (lax.axis_index("dp") % 2).astype(jnp.int32).reshape(1)
        me = lax.axis_index("space").astype(jnp.int32).reshape(1)
        edges = exchange(jnp.broadcast_to(adjacency.reshape(1, 36), (peers, 36)), "space")
        taps = kernels.reshape(2, 9, depth, CH)
        mine, theirs = gather(taps)
        send1, routes = pack(me, edges, field)
        got1 = trade(send1)
        part1, kernel1 = conv(core, field, mine, theirs, 0, False)
        state1, slope1, send2 = finish(routes, part1, field, got1, kernel1)
        got2 = trade(send2)
        part2, kernel2, turned2 = conv(core, state1, mine, theirs, 1, True)
        state2, grad2, send3, triples2 = last(routes, part2, state1, got2, kernel2, turned2, cot)
        returned = trade(send3)
        back, kept2, given2 = second(
            routes, core, state1, grad2, got2, triples2, turned2, pairs, depth
        )
        blocks2, back = lax.optimization_barrier((halve(kept2, given2), back))
        layer2 = exchange(blocks2, ("dp", "space"), same_core_all)
        kept1, given1 = first(routes, core, field, cot, back, slope1, got1, returned, pairs, depth)
        layer1 = exchange(halve(kept1, given1), ("dp", "space"), same_core_all)
        summed = sum_all((layer1, layer2), peers)
        grads = join(exchange(summed, "space"), depth)
        return state2[None], grads.reshape(2, 3, 3, depth, CH)

    in_specs = (
        P("dp", "space", None, None, None),
        P(None, None, None, "dp", None),
        P("dp", "space", None, None, None),
        P("space", None, None),
    )
    out_specs = (P("dp", "space", None, None, None), P(None, None, None, "dp", None))
    return jax.shard_map(
        per_device, mesh=mesh, in_specs=in_specs, out_specs=out_specs, check_vma=False
    )
```

time: 439 us -> 195 us (0.44); the launches traced: 433 us -> 194 us
  waiting for transfers between devices: 224 us -> 25.1 us
  matrix products: 109 us -> 0 us
  Pallas kernels: 0 us -> 81.1 us
  blocking collectives: 0 us -> 56.5 us
  local copies, waits for them, and re-layouts: 43.6 us -> 8.11 us
  other arithmetic: 20 us -> 0 us
  between operations: 15.1 us -> 0.78 us
    unnamed x3 -> x0, waiting for transfers between devices: 153 us -> none
    dot_general x45 -> x0, matrix products: 109 us -> none  [the longest x18 52.3 us: convolve(): jnp.dot(patches, kernel[row_off, col_off], preferred_element_type=jnp.flo...]
    pallas_call x0 -> x11, Pallas kernels: none -> 81.1 us  [the longest x2 20.1 us: conv(): pl.pallas_call(lambda *refs: conv_kernel(turned, shards, *refs), name='co...]
    all_to_all x0 -> x3, blocking collectives: none -> 56.5 us  [exchange(): lax.all_to_all(value, axes, 0, 0, tiled=True, axis_index_groups=groups)]
    all_to_all x5, waiting for transfers between devices: 62.2 us -> 22.8 us  [exchange(): lax.all_to_all(value, axes, 0, 0, tiled=True, axis_index_groups=groups)]
    dot_general x3 -> x0, local copies, waits for them, and re-layouts: 11 us -> none  [convolve(): jnp.dot(patches, kernel[row_off, col_off], preferred_element_type=jnp.flo...]
    all_gather x1 -> x0, waiting for transfers between devices: 8.55 us -> none  [per_device(): weights = lax.all_gather(kernels, 'dp', axis=3, tiled=True)]
    unnamed x91 -> x20, local copies, waits for them, and re-layouts: 14.6 us -> 6.3 us
  transfers between devices with their start and end apart: 7 -> 8, of which waited for: 7 -> 5; matrix products, arithmetic and copies ran while one was open for 7% -> 0% of each run, Pallas kernels for 0% -> 24%
where the time goes in v1:
time: 195 us; the launch traced here: 194 us
  Pallas kernels  81.1 us (42%)
  blocking collectives  56.5 us (29%)
  waiting for transfers between devices  25.1 us (13%)
  starting transfers between devices  22.7 us (12%)
  local copies, waits for them, and re-layouts  8.11 us (4%)
    all_to_all x3, blocking collectives, exchange(): lax.all_to_all(value, axes, 0, 0, tiled=True, axis_index_groups=groups)  56.5 us
    all_to_all x5, waiting for transfers between devices, exchange(): lax.all_to_all(value, axes, 0, 0, tiled=True, axis_index_groups=groups)  22.8 us
    all_to_all x5, starting transfers between devices, exchange(): lax.all_to_all(value, axes, 0, 0, tiled=True, axis_index_groups=groups)  22.5 us
    pallas_call x2, Pallas kernels, conv(): pl.pallas_call(lambda *refs: conv_kernel(turned, shards, *refs), name='co...  20.1 us
    pallas_call x1, Pallas kernels, second(): pl.pallas_call(second_kernel, name='second', out_shape=(struct((TILES * C...  17.6 us
    pallas_call x1, Pallas kernels, first(): pl.pallas_call(first_kernel, name='first', out_shape=(struct(half, F32),...  13.8 us
    pallas_call x1, Pallas kernels, last(): pl.pallas_call(last_kernel, name='last', out_shape=(struct(field.shape, B...  9.23 us
    pallas_call x1, Pallas kernels, finish(): pl.pallas_call(finish_kernel, name='finish', out_shape=(struct(field.shap...  8.31 us
  transfers between devices with their start and end apart: 8, of which 5 were waited for; matrix products, arithmetic and copies ran while one was open for 0% of the time, Pallas kernels for 24%

profile of v1, /device:TPU:0, one launch (start us, length us, event | category | flops | bytes accessed | tf_op | source)
XLA Modules:
  0.0 194.3 jit_solution(9245780190678634296)
XLA Ops:
  0.6 0.0 copy-start.8
  0.6 1.0 broadcast_in_dim.20
  1.7 26.3 %all_to_all.43.refs_2_ = bf16[8,2,9,16,256]{4,3,2,1,0:T(8,128)(2,1)S(1)} all-to-all(bf16[8,2,9,16,256]{4,3,2,1,0:T(8,128)(2,1)S(1)} %broadcast_in_dim.20), channel_id=1, replica_groups={{0,16,32,48,64,80,96,112},{8,24,40,56,72,88,104,120},{1,17,33,49,65,81,..., dimensions={0} | all-to-all | bytes 2359296 | tf_op jit(solution)/shard_map/all_to_all | solution.py:699
  28.0 0.0 copy-start.3
  28.0 0.0 collective-permute-start
  28.0 0.0 copy-done.8
  28.0 0.1 broadcast_in_dim.17
  28.1 0.7 broadcast_in_dim.18
  28.8 4.6 %all-to-all-start = ((s32[8,1,36]{2,1,0:T(1,128)}), s32[8,1,36]{2,1,0:T(1,128)S(1)}, u32[]{:S(2)}, u32[]{:S(2)}) async-start(s32[8,1,36]{2,1,0:T(1,128)} %broadcast_in_dim.18), calls=%async_computation | async-start | bytes 8192 | tf_op jit(solution)/shard_map/all_to_all | solution.py:699
  33.4 6.1 %all-to-all-done = s32[8,1,36]{2,1,0:T(1,128)S(1)} async-done(((s32[8,1,36]{2,1,0:T(1,128)}), s32[8,1,36]{2,1,0:T(1,128)S(1)}, u32[]{:S(2)}, u32[]{:S(2)}) %all-to-all-start) | async-done | bytes 1184 | tf_op jit(solution)/shard_map/all_to_all | solution.py:699
  39.5 0.0 copy-start.7
  39.5 0.6 copy-done.7
  40.1 3.2 %pack.1 = (bf16[56,32,256]{2,1,0:T(8,128)(2,1)}, s32[88]{0:T(128)}) custom-call(s32[1]{0:T(128)} %bitcast.me_ref, s32[8,36]{1,0:T(8,128)} %bitcast.30, bf16[3,32,32,256]{3,2,1,0:T(8,128)(2,1)} %bitcast.14), custom_call_target="tpu_custom_call" | custom-call | bytes 3000000 | tf_op jit(solution)/shard_map/pack/pallas_call | solution.py:99
  43.3 0.0 copy-done.3
  43.3 3.6 %all-to-all-start.2 = ((bf16[8,7,32,256]{3,2,1,0:T(8,128)(2,1)}), bf16[8,7,32,256]{3,2,1,0:T(8,128)(2,1)S(1)}, u32[]{:S(2)}, u32[]{:S(2)}) async-start(bf16[8,7,32,256]{3,2,1,0:T(8,128)(2,1)} %bitcast.24), calls=%async_computation.2 | async-start | bytes 1835008 | tf_op jit(solution)/shard_map/all_to_all | solution.py:699
  46.8 0.0 collective-permute-done.refs_3_
  46.9 0.0 copy-start.9
  46.9 1.1 copy-done.9
  48.0 9.7 %conv.1 = (f32[3072,256]{1,0:T(8,128)}, bf16[2304,256]{1,0:T(8,128)(2,1)}) custom-call(s32[1]{0:T(128)} %bitcast.3.refs_0_.core_ref, bf16[3,32,32,256]{3,2,1,0:T(8,128)(2,1)} %bitcast.15, bf16[8,2,9,16,256]{4,3,2,1,0:T(8,128)(2,1)} %copy-done.3, bf16[8,2,9,16,256]{4,3,2,1,0:T(8,128)(2,1)} %copy-done.9), custom_call_target="tpu_custom_call" | custom-call | flops 3600000000 | bytes 7000000 | tf_op jit(solution)/shard_map/conv/pallas_call | solution.py:212
  57.6 2.9 %all-to-all-done.2 = bf16[8,7,32,256]{3,2,1,0:T(8,128)(2,1)S(1)} async-done(((bf16[8,7,32,256]{3,2,1,0:T(8,128)(2,1)}), bf16[8,7,32,256]{3,2,1,0:T(8,128)(2,1)S(1)}, u32[]{:S(2)}, u32[]{:S(2)}) %all-to-all-start.2) | async-done | bytes 917536 | tf_op jit(solution)/shard_map/all_to_all | solution.py:699
  60.5 1.0 copy-done.1
  61.5 8.3 %finish.1 = (bf16[3,32,32,256]{3,2,1,0:T(8,128)(2,1)}, f32[3072,256]{1,0:T(8,128)}, bf16[56,32,256]{2,1,0:T(8,128)(2,1)}) custom-call(s32[88]{0:T(128)} %get-tuple-element.23.routes_ref, f32[3072,256]{1,0:T(8,128)} %get-tuple-element.24.part_ref, bf16[3,32,32,256]{3,2,1,0:T(8,128)(2,1)} %bitcast.16, bf16[56,32,256]{2,1,0:T(8,128)(2,1)} %bitcast.20, ...), custom_call_target="tpu_custom_call" | custom-call | flops 200000000 | bytes 10000000 | tf_op jit(solution)/shard_map/finish/pallas_call | solution.py:296
  69.8 3.6 %all-to-all-start.3 = ((bf16[8,7,32,256]{3,2,1,0:T(8,128)(2,1)}), bf16[8,7,32,256]{3,2,1,0:T(8,128)(2,1)S(1)}, u32[]{:S(2)}, u32[]{:S(2)}) async-start(bf16[8,7,32,256]{3,2,1,0:T(8,128)(2,1)} %bitcast.27), calls=%async_computation.3 | async-start | bytes 1835008 | tf_op jit(solution)/shard_map/all_to_all | solution.py:699
  73.3 10.4 %conv_turned.1 = (f32[3072,256]{1,0:T(8,128)}, bf16[2304,256]{1,0:T(8,128)(2,1)}, bf16[2304,256]{1,0:T(8,128)(2,1)}) custom-call(s32[1]{0:T(128)} %bitcast.3.refs_0_.core_ref, bf16[3,32,32,256]{3,2,1,0:T(8,128)(2,1)} %get-tuple-element.27.refs_1_.field_ref, bf16[8,2,9,16,256]{4,3,2,1,0:T(8,128)(2,1)} %copy-done.3, bf16[8,2,9,16,256]{4,3,2,1,0:T(8,128)(2,1)} %copy-done.9), custom_call_target="tpu_custom_call" | custom-call | flops 3600000000 | bytes 7000000 | tf_op jit(solution)/shard_map/conv_turned/pallas_call | solution.py:212
  83.7 2.6 %all-to-all-done.3 = bf16[8,7,32,256]{3,2,1,0:T(8,128)(2,1)S(1)} async-done(((bf16[8,7,32,256]{3,2,1,0:T(8,128)(2,1)}), bf16[8,7,32,256]{3,2,1,0:T(8,128)(2,1)S(1)}, u32[]{:S(2)}, u32[]{:S(2)}) %all-to-all-start.3) | async-done | bytes 917536 | tf_op jit(solution)/shard_map/all_to_all | solution.py:699
  86.3 0.9 copy-done
  87.3 9.2 %last.1 = (bf16[3,32,32,256]{3,2,1,0:T(8,128)(2,1)}, bf16[3072,256]{1,0:T(8,128)(2,1)}, bf16[56,32,256]{2,1,0:T(8,128)(2,1)}, bf16[4,96,768]{2,1,0:T(8,128)(2,1)}) custom-call(s32[88]{0:T(128)} %get-tuple-element.23.routes_ref, f32[3072,256]{1,0:T(8,128)} %get-tuple-element.28.part_ref, bf16[3,32,32,256]{3,2,1,0:T(8,128)(2,1)} %get-tuple-element.27.refs_1_.field_ref, ...), custom_call_target="tpu_custom_call" | custom-call | flops 400000000 | bytes 12000000 | tf_op jit(solution)/shard_map/last/pallas_call | solution.py:390
  96.5 3.6 %all-to-all-start.4 = ((bf16[8,7,32,256]{3,2,1,0:T(8,128)(2,1)}), bf16[8,7,32,256]{3,2,1,0:T(8,128)(2,1)S(1)}, u32[]{:S(2)}, u32[]{:S(2)}) async-start(bf16[8,7,32,256]{3,2,1,0:T(8,128)(2,1)} %bitcast.26), calls=%async_computation.4 | async-start | bytes 1835008 | tf_op jit(solution)/shard_map/all_to_all | solution.py:699
  100.1 17.6 %second.1 = (f32[3072,256]{1,0:T(8,128)}, f32[8,9,16,256]{3,2,1,0:T(8,128)}, bf16[8,9,16,256]{3,2,1,0:T(8,128)(2,1)}) custom-call(s32[88]{0:T(128)} %get-tuple-element.23.routes_ref, s32[1]{0:T(128)} %bitcast.3.refs_0_.core_ref, bf16[3,32,32,256]{3,2,1,0:T(8,128)(2,1)} %get-tuple-element.27.refs_1_.field_ref, bf16[3072,256]{1,0:T(8,128)(2,1)} %get-tuple-element.33.grad_ref, ...), custom_call_target="tpu_custom_call" | custom-call | flops 7200000000 | bytes 12000000 | tf_op jit(solution)/shard_map/second/pallas_call | solution.py:510
  117.7 0.0 collective-permute-start.1
  117.8 2.2 %collective-permute-done.1.got_ref = bf16[8,9,16,256]{3,2,1,0:T(8,128)(2,1)S(1)} collective-permute-done((bf16[8,9,16,256]{3,2,1,0:T(8,128)(2,1)}, bf16[8,9,16,256]{3,2,1,0:T(8,128)(2,1)S(1)}, u32[]{:S(2)}, u32[]{:S(2)}) %collective-permute-start.1) | collective-permute-done | bytes 589856 | tf_op jit(solution)/shard_map/ppermute | solution.py:722
  120.0 0.8 copy-done.6
  120.8 2.5 %cut.2 = bf16[64,36,128]{2,1,0:T(8,128)(2,1)} custom-call(f32[8,9,16,256]{3,2,1,0:T(8,128)} %get-tuple-element.35.kept_ref, bf16[8,9,16,256]{3,2,1,0:T(8,128)(2,1)} %copy-done.6), custom_call_target="tpu_custom_call" | custom-call | bytes 3000000 | tf_op jit(solution)/shard_map/cut/pallas_call | solution.py:638
  123.3 0.0 all-to-all-done.4
  123.3 1.0 copy-done.4
  124.4 13.8 %first.1 = (f32[8,9,16,256]{3,2,1,0:T(8,128)}, bf16[8,9,16,256]{3,2,1,0:T(8,128)(2,1)}) custom-call(s32[88]{0:T(128)} %get-tuple-element.23.routes_ref, s32[1]{0:T(128)} %bitcast.3.refs_0_.core_ref, bf16[3,32,32,256]{3,2,1,0:T(8,128)(2,1)} %bitcast.17, bf16[3,32,32,256]{3,2,1,0:T(8,128)(2,1)} %bitcast.23, f32[3072,256]{1,0:T(8,128)} %get-tuple-element.38.back_ref, ...), custom_call_target="tpu_custom_call" | custom-call | flops 3600000000 | bytes 12000000 | tf_op jit(solution)/shard_map/first/pallas_call | solution.py:592
  138.2 0.1 collective-permute-start.2
  138.3 7.2 %all-to-all-start.6 = ((bf16[64,36,128]{2,1,0:T(8,128)(2,1)}), bf16[64,36,128]{2,1,0:T(8,128)(2,1)S(1)}, u32[]{:S(2)}, u32[]{:S(2)}) async-start(bf16[64,36,128]{2,1,0:T(8,128)(2,1)} %cut.2), calls=%async_computation.6 | async-start | bytes 1310720 | tf_op jit(solution)/shard_map/all_to_all | solution.py:699
  145.5 0.0 collective-permute-done.2.got_ref
  145.5 0.0 copy-start.5
  145.5 0.8 copy-done.5
  146.3 2.5 %cut.3 = bf16[64,36,128]{2,1,0:T(8,128)(2,1)} custom-call(f32[8,9,16,256]{3,2,1,0:T(8,128)} %get-tuple-element.41.kept_ref, bf16[8,9,16,256]{3,2,1,0:T(8,128)(2,1)} %copy-done.5), custom_call_target="tpu_custom_call" | custom-call | bytes 3000000 | tf_op jit(solution)/shard_map/cut/pallas_call | solution.py:638
  148.8 11.3 %all-to-all-done.6.refs_1_ = bf16[64,36,128]{2,1,0:T(8,128)(2,1)S(1)} async-done(((bf16[64,36,128]{2,1,0:T(8,128)(2,1)}), bf16[64,36,128]{2,1,0:T(8,128)(2,1)S(1)}, u32[]{:S(2)}, u32[]{:S(2)}) %all-to-all-start.6) | async-done | bytes 589856 | tf_op jit(solution)/shard_map/all_to_all | solution.py:699
  160.1 18.6 %all_to_all.44.refs_0_ = bf16[64,36,128]{2,1,0:T(8,128)(2,1)} all-to-all(bf16[64,36,128]{2,1,0:T(8,128)(2,1)} %cut.3), channel_id=1, replica_groups={{0,1,2,3,4,5,6,7,16,17,18,19,20,21,22,23,32,33,34,35,36,37,38,39,48,49,..., dimensions={0} | all-to-all | bytes 1179648 | tf_op jit(solution)/shard_map/all_to_all | solution.py:699
  178.7 0.0 copy-done.2
  178.7 2.2 %sum_all.1 = f32[8,72,128]{2,1,0:T(8,128)} custom-call(bf16[64,36,128]{2,1,0:T(8,128)(2,1)} %all_to_all.44.refs_0_, bf16[64,36,128]{2,1,0:T(8,128)(2,1)} %copy-done.2), custom_call_target="tpu_custom_call" | custom-call | bytes 2000000 | tf_op jit(solution)/shard_map/sum_all/pallas_call | solution.py:662
  180.9 11.7 %all_to_all.45.in_ref = f32[8,72,128]{2,1,0:T(8,128)} all-to-all(f32[8,72,128]{2,1,0:T(8,128)} %sum_all.1), channel_id=1, replica_groups=mesh['dp'=16,'space'=8] {'space'}, dimensions={0} | all-to-all | bytes 589824 | tf_op jit(solution)/shard_map/all_to_all | solution.py:699
  192.6 1.7 join.1
  (5 shorter events, 0.0 us)
Async XLA Ops:
  0.6 27.3 %copy-start.8 = (s32[3,4,3]{2,1,0:T(4,128)S(1)}, s32[3,4,3]{2,1,0:T(4,128)}, u32[]{:S(2)}) copy-start(s32[3,4,3]{2,1,0:T(4,128)} %param.7) | copy-start | bytes 436
  28.0 15.3 %copy-start.3 = (bf16[8,2,9,16,256]{4,3,2,1,0:T(8,128)(2,1)}, bf16[8,2,9,16,256]{4,3,2,1,0:T(8,128)(2,1)S(1)}, u32[]{:S(2)}) copy-start(bf16[8,2,9,16,256]{4,3,2,1,0:T(8,128)(2,1)S(1)} %all_to_all.43.refs_2_) | copy-start | bytes 3538948
  28.0 18.9 %collective-permute-start = (bf16[8,2,9,16,256]{4,3,2,1,0:T(8,128)(2,1)S(1)}, bf16[8,2,9,16,256]{4,3,2,1,0:T(8,128)(2,1)S(1)}, u32[]{:S(2)}, u32[]{:S(2)}) collective-permute-start(bf16[8,2,9,16,256]{4,3,2,1,0:T(8,128)(2,1)S(1)} %all_to_all.43.refs_2_), channel_id=1, source_target_pairs={{0,8},{8,0},{16,24},{24,16},{32,40},{40,32},{48,56},{56,48},{64,72... | collective-permute-start | bytes 3538952 | tf_op jit(solution)/shard_map/ppermute | solution.py:716
  28.8 10.7 %all-to-all-start = ((s32[8,1,36]{2,1,0:T(1,128)}), s32[8,1,36]{2,1,0:T(1,128)S(1)}, u32[]{:S(2)}, u32[]{:S(2)}) async-start(s32[8,1,36]{2,1,0:T(1,128)} %broadcast_in_dim.18), calls=%async_computation | async-start | bytes 8192 | tf_op jit(solution)/shard_map/all_to_all | solution.py:699
  39.5 0.6 copy-start.7
  43.3 17.2 %all-to-all-start.2 = ((bf16[8,7,32,256]{3,2,1,0:T(8,128)(2,1)}), bf16[8,7,32,256]{3,2,1,0:T(8,128)(2,1)S(1)}, u32[]{:S(2)}, u32[]{:S(2)}) async-start(bf16[8,7,32,256]{3,2,1,0:T(8,128)(2,1)} %bitcast.24), calls=%async_computation.2 | async-start | bytes 1835008 | tf_op jit(solution)/shard_map/all_to_all | solution.py:699
  46.9 1.1 copy-start.9
  60.5 1.0 copy-start.1
  69.8 16.6 %all-to-all-start.3 = ((bf16[8,7,32,256]{3,2,1,0:T(8,128)(2,1)}), bf16[8,7,32,256]{3,2,1,0:T(8,128)(2,1)S(1)}, u32[]{:S(2)}, u32[]{:S(2)}) async-start(bf16[8,7,32,256]{3,2,1,0:T(8,128)(2,1)} %bitcast.27), calls=%async_computation.3 | async-start | bytes 1835008 | tf_op jit(solution)/shard_map/all_to_all | solution.py:699
  86.3 0.9 copy-start
  96.5 26.8 %all-to-all-start.4 = ((bf16[8,7,32,256]{3,2,1,0:T(8,128)(2,1)}), bf16[8,7,32,256]{3,2,1,0:T(8,128)(2,1)S(1)}, u32[]{:S(2)}, u32[]{:S(2)}) async-start(bf16[8,7,32,256]{3,2,1,0:T(8,128)(2,1)} %bitcast.26), calls=%async_computation.4 | async-start | bytes 1835008 | tf_op jit(solution)/shard_map/all_to_all | solution.py:699
  117.7 2.3 %collective-permute-start.1 = (bf16[8,9,16,256]{3,2,1,0:T(8,128)(2,1)}, bf16[8,9,16,256]{3,2,1,0:T(8,128)(2,1)S(1)}, u32[]{:S(2)}, u32[]{:S(2)}) collective-permute-start(bf16[8,9,16,256]{3,2,1,0:T(8,128)(2,1)} %get-tuple-element.36), channel_id=1, source_target_pairs={{0,8},{8,0},{16,24},{24,16},{32,40},{40,32},{48,56},{56,48},{64,72... | collective-permute-start | bytes 1769480 | tf_op jit(solution)/shard_map/ppermute | solution.py:722
  120.0 0.8 copy-start.6
  123.3 1.0 copy-start.4
  138.2 7.3 %collective-permute-start.2 = (bf16[8,9,16,256]{3,2,1,0:T(8,128)(2,1)}, bf16[8,9,16,256]{3,2,1,0:T(8,128)(2,1)S(1)}, u32[]{:S(2)}, u32[]{:S(2)}) collective-permute-start(bf16[8,9,16,256]{3,2,1,0:T(8,128)(2,1)} %get-tuple-element.42), channel_id=1, source_target_pairs={{0,8},{8,0},{16,24},{24,16},{32,40},{40,32},{48,56},{56,48},{64,72... | collective-permute-start | bytes 1769480 | tf_op jit(solution)/shard_map/ppermute | solution.py:722
  138.3 21.8 %all-to-all-start.6 = ((bf16[64,36,128]{2,1,0:T(8,128)(2,1)}), bf16[64,36,128]{2,1,0:T(8,128)(2,1)S(1)}, u32[]{:S(2)}, u32[]{:S(2)}) async-start(bf16[64,36,128]{2,1,0:T(8,128)(2,1)} %cut.2), calls=%async_computation.6 | async-start | bytes 1310720 | tf_op jit(solution)/shard_map/all_to_all | solution.py:699
  145.5 0.8 copy-start.5
  160.1 18.6 %copy-start.2 = (bf16[64,36,128]{2,1,0:T(8,128)(2,1)}, bf16[64,36,128]{2,1,0:T(8,128)(2,1)S(1)}, u32[]{:S(2)}) copy-start(bf16[64,36,128]{2,1,0:T(8,128)(2,1)S(1)} %all-to-all-done.6.refs_1_) | copy-start | bytes 1769476

commit v2 on v1

--- a/solution.py
+++ b/solution.py
@@ -180,8 +180,9 @@
         clear_margin(wide)
         for pair in range(shards // 2):
             for source, side in ((mine_ref, core), (theirs_ref, 1 - core)):
+                base = (core_ref[1] ^ pair) * 2 * depth + side * depth
                 for tap in range(9):
-                    at = pl.multiple_of(tap * CH + pair * 2 * depth + side * depth, depth)
+                    at = pl.multiple_of(tap * CH + base, depth)
                     kernel_ref[pl.ds(at, depth), :] = source[pair, 0, tap]
         if turned:
             for tap in range(9):
@@ -618,56 +619,55 @@
     )(routes, core, field, cotangent, back, slope, got, returned)
 
 
-def cut_kernel(kept_ref, got_ref, out_ref, rows):
-    pairs, _, depth, _ = kept_ref.shape
+def cut_kernel(kept1_ref, got1_ref, kept2_ref, got2_ref, out_ref, rows):
+    depth = kept1_ref.shape[2]
     run = 9 * depth // 4
-    for pair in range(pairs):
+    for layer, (kept_ref, got_ref) in enumerate(((kept1_ref, got1_ref), (kept2_ref, got2_ref))):
         for tap in range(9):
-            rows[tap * depth : (tap + 1) * depth, :] = kept_ref[pair, tap] + got_ref[
-                pair, tap
+            rows[layer, tap * depth : (tap + 1) * depth, :] = kept_ref[0, tap] + got_ref[
+                0, tap
             ].astype(F32)
         for peer in range(8):
             high, low = divmod(peer, 4)
-            out_ref[pair * 8 + peer] = rows[
-                low * run : (low + 1) * run, high * 128 : (high + 1) * 128
+            out_ref[peer, layer * run : (layer + 1) * run, :] = rows[
+                layer, low * run : (low + 1) * run, high * 128 : (high + 1) * 128
             ].astype(BF)
 
 
-def cut(kept, got):
-    pairs, _, depth, _ = kept.shape
+def cut(kept1, got1, kept2, got2):
+    pairs, _, depth, _ = kept1.shape
+    run = 9 * depth // 4
     return pl.pallas_call(
         cut_kernel,
         name="cut",
-        out_shape=struct((pairs * 8, 9 * depth // 4, 128), BF),
-        in_specs=[vmem(), vmem()],
-        out_specs=vmem(),
-        scratch_shapes=[pltpu.VMEM((9 * depth, CH), F32)],
-        compiler_params=params(),
-        cost_estimate=cost(0, 3_000_000),
-    )(kept, got)
-
-
-def sum_kernel(*refs):
-    *in_refs, out_ref = refs
-    for layer, source in enumerate(in_refs):
-        summed = source[0].astype(F32)
-        for other in range(1, source.shape[0]):
-            summed = summed + source[other].astype(F32)
-        for peer in range(out_ref.shape[0]):
-            run = summed.shape[0]
-            out_ref[peer, layer * run : (layer + 1) * run] = summed
+        out_shape=struct((pairs * 8, 2 * run, 128), BF),
+        grid=(pairs,),
+        in_specs=[per_tile(1, 9, depth, CH)] * 4,
+        out_specs=per_tile(8, 2 * run, 128),
+        scratch_shapes=[pltpu.VMEM((2, 9 * depth, CH), F32)],
+        compiler_params=params(1),
+        cost_estimate=cost(0, 6_000_000),
+    )(kept1, got1, kept2, got2)
+
+
+def sum_kernel(in_ref, out_ref):
+    summed = in_ref[0].astype(F32)
+    for other in range(1, in_ref.shape[0]):
+        summed = summed + in_ref[other].astype(F32)
+    for peer in range(out_ref.shape[0]):
+        out_ref[peer] = summed
 
 
 def sum_all(parts, peers):
     return pl.pallas_call(
         sum_kernel,
         name="sum_all",
-        out_shape=struct((peers, len(parts) * parts[0].shape[1], 128), F32),
-        in_specs=[vmem()] * len(parts),
+        out_shape=struct((peers, *parts.shape[1:]), F32),
+        in_specs=[vmem()],
         out_specs=vmem(),
         compiler_params=params(),
         cost_estimate=cost(0, 2_000_000),
-    )(*parts)
+    )(parts)
 
 
 def join_kernel(in_ref, out_ref):
@@ -702,7 +702,6 @@
 def solution(mesh):
     shards, peers = mesh.shape["dp"], mesh.shape["space"]
     pairs, depth = shards // 2, CH // shards
-    same_core = [[pair * 2 + core for pair in range(pairs)] for core in range(2)]
     same_core_all = [
         [(pair * 2 + core) * peers + peer for pair in range(pairs) for peer in range(peers)]
         for core in range(2)
@@ -710,27 +709,28 @@
     swap = [(index, index ^ 1) for index in range(shards)]
 
     def gather(shard):
-        mine = exchange(
-            jnp.broadcast_to(shard[None], (pairs, *shard.shape)), "dp", same_core
-        )
-        return mine, lax.ppermute(mine, "dp", swap)
+        blocks = []
+        for step in range(1, pairs):
+            route = [(index, index ^ (2 * step)) for index in range(shards)]
+            blocks.append(lax.ppermute(shard, "dp", route))
+        return blocks
 
     def trade(strips):
         return exchange(strips.reshape(peers, SLOTS, SIDE, CH), "space").reshape(strips.shape)
 
-    def halve(kept, given):
-        return cut(kept, lax.ppermute(given, "dp", swap))
-
     def per_device(inputs, kernels, cotangent, adjacency):
+        place = lax.axis_index("dp").astype(jnp.int32)
+        core = jnp.stack([place % 2, place // 2])
+        me = lax.axis_index("space").astype(jnp.int32).reshape(1)
+        edges = exchange(jnp.broadcast_to(adjacency.reshape(1, 36), (peers, 36)), "space")
+        blocks = gather(kernels.reshape(2, 9, depth, CH))
         field = inputs[0]
         cot = cotangent[0]
-        core = (lax.axis_index("dp") % 2).astype(jnp.int32).reshape(1)
-        me = lax.axis_index("space").astype(jnp.int32).reshape(1)
-        edges = exchange(jnp.broadcast_to(adjacency.reshape(1, 36), (peers, 36)), "space")
-        taps = kernels.reshape(2, 9, depth, CH)
-        mine, theirs = gather(taps)
         send1, routes = pack(me, edges, field)
+        own, send1 = lax.optimization_barrier((kernels.reshape(2, 9, depth, CH), send1))
         got1 = trade(send1)
+        mine = jnp.stack([own, *blocks])
+        theirs = lax.ppermute(mine, "dp", swap)
         part1, kernel1 = conv(core, field, mine, theirs, 0, False)
         state1, slope1, send2 = finish(routes, part1, field, got1, kernel1)
         got2 = trade(send2)
@@ -740,11 +740,12 @@
         back, kept2, given2 = second(
             routes, core, state1, grad2, got2, triples2, turned2, pairs, depth
         )
-        blocks2, back = lax.optimization_barrier((halve(kept2, given2), back))
-        layer2 = exchange(blocks2, ("dp", "space"), same_core_all)
-        kept1, given1 = first(routes, core, field, cot, back, slope1, got1, returned, pairs, depth)
-        layer1 = exchange(halve(kept1, given1), ("dp", "space"), same_core_all)
-        summed = sum_all((layer1, layer2), peers)
+        got_half2 = lax.ppermute(given2, "dp", swap)
+        kept1, given1 = first(
+            routes, core, field, cot, back, slope1, got1, returned, pairs, depth
+        )
+        blocks = cut(kept1, lax.ppermute(given1, "dp", swap), kept2, got_half2)
+        summed = sum_all(exchange(blocks, ("dp", "space"), same_core_all), peers)
         grads = join(exchange(summed, "space"), depth)
         return state2[None], grads.reshape(2, 3, 3, depth, CH)
 

time: 195 us -> 188 us (0.964)
  blocking collectives: 56.5 us -> 40.2 us
  starting transfers between devices: 22.7 us -> 35.6 us
  waiting for transfers between devices: 25.1 us -> 20.6 us
    ppermute x3 -> x10, starting transfers between devices: 0.19 us -> 17.9 us  [the longest x7 17.3 us: gather(): blocks.append(lax.ppermute(shard, 'dp', route))]
    all_to_all x3 -> x2, blocking collectives: 56.5 us -> 40.2 us  [exchange(): lax.all_to_all(value, axes, 0, 0, tiled=True, axis_index_groups=groups)]
    all_to_all x5 -> x4, waiting for transfers between devices: 22.8 us -> 7.07 us  [exchange(): lax.all_to_all(value, axes, 0, 0, tiled=True, axis_index_groups=groups)]
    ppermute x3 -> x10, waiting for transfers between devices: 2.21 us -> 13.6 us  [the longest x7 11.7 us: gather(): blocks.append(lax.ppermute(shard, 'dp', route))]
    all_to_all x5 -> x4, starting transfers between devices: 22.5 us -> 17.6 us  [exchange(): lax.all_to_all(value, axes, 0, 0, tiled=True, axis_index_groups=groups)]
    pallas_call x3 -> x2, Pallas kernels: 7.27 us -> 8.22 us  [the longest x1 6.04 us: cut(): pl.pallas_call(cut_kernel, name='cut', out_shape=struct((pairs * 8, 2 * r...]
    unnamed x20 -> x25, local copies, waits for them, and re-layouts: 6.3 us -> 5.4 us
  transfers between devices with their start and end apart: 8 -> 14, of which waited for: 5 -> 6; matrix products, arithmetic and copies ran while one was open for 0% -> 0% of each run, Pallas kernels for 24% -> 29%
where the time goes in v2:
time: 188 us; the launch traced here: 187 us
  Pallas kernels  82.5 us (44%)
  blocking collectives  40.2 us (21%)
  starting transfers between devices  35.6 us (19%)
  waiting for transfers between devices  20.6 us (11%)
  local copies, waits for them, and re-layouts  6.82 us (4%)
    all_to_all x2, blocking collectives, exchange(): lax.all_to_all(value, axes, 0, 0, tiled=True, axis_index_groups=groups)  40.2 us
    pallas_call x2, Pallas kernels, conv(): pl.pallas_call(lambda *refs: conv_kernel(turned, shards, *refs), name='co...  20.3 us
    pallas_call x1, Pallas kernels, second(): pl.pallas_call(second_kernel, name='second', out_shape=(struct((TILES * C...  17.7 us
    all_to_all x4, starting transfers between devices, exchange(): lax.all_to_all(value, axes, 0, 0, tiled=True, axis_index_groups=groups)  17.6 us
    ppermute x7, starting transfers between devices, gather(): blocks.append(lax.ppermute(shard, 'dp', route))  17.3 us
    pallas_call x1, Pallas kernels, first(): pl.pallas_call(first_kernel, name='first', out_shape=(struct(half, F32),...  13.9 us
    ppermute x7, waiting for transfers between devices, gather(): blocks.append(lax.ppermute(shard, 'dp', route))  11.7 us
    pallas_call x1, Pallas kernels, last(): pl.pallas_call(last_kernel, name='last', out_shape=(struct(field.shape, B...  9.23 us
  transfers between devices with their start and end apart: 14, of which 6 were waited for; matrix products, arithmetic and copies ran while one was open for 0% of the time, Pallas kernels for 29%

profile of v2, /device:TPU:0, one launch (start us, length us, event | category | flops | bytes accessed | tf_op | source)
XLA Modules:
  0.0 187.1 jit_solution(4372115401444379109)
XLA Ops:
  0.6 0.0 copy-start.5
  0.6 0.8 broadcast_in_dim.10
  1.5 0.6 broadcast_in_dim.11
  2.1 5.5 %all-to-all-start = ((s32[8,1,36]{2,1,0:T(1,128)}), s32[8,1,36]{2,1,0:T(1,128)S(1)}, u32[]{:S(2)}, u32[]{:S(2)}) async-start(s32[8,1,36]{2,1,0:T(1,128)} %broadcast_in_dim.11), calls=%async_computation | async-start | bytes 8192 | tf_op jit(solution)/shard_map/all_to_all | solution.py:699
  7.6 6.2 %collective-permute-start.6 = (bf16[2,9,16,256]{3,2,1,0:T(8,128)(2,1)}, bf16[2,9,16,256]{3,2,1,0:T(8,128)(2,1)S(1)}, u32[]{:S(2)}, u32[]{:S(2)}) collective-permute-start(bf16[2,9,16,256]{3,2,1,0:T(8,128)(2,1)} %bitcast.45), channel_id=1, source_target_pairs={{0,112},{8,120},{16,96},{24,104},{32,80},{40,88},{48,64},{56,72},{... | collective-permute-start | bytes 442376 | tf_op jit(solution)/shard_map/ppermute | solution.py:715
  13.8 0.2 collective-permute-start.5
  14.0 2.3 %collective-permute-start.4 = (bf16[2,9,16,256]{3,2,1,0:T(8,128)(2,1)}, bf16[2,9,16,256]{3,2,1,0:T(8,128)(2,1)S(1)}, u32[]{:S(2)}, u32[]{:S(2)}) collective-permute-start(bf16[2,9,16,256]{3,2,1,0:T(8,128)(2,1)} %bitcast.47), channel_id=1, source_target_pairs={{0,80},{8,88},{16,64},{24,72},{32,112},{40,120},{48,96},{56,104},{... | collective-permute-start | bytes 442376 | tf_op jit(solution)/shard_map/ppermute | solution.py:715
  16.2 1.5 collective-permute-start.3
  17.7 1.3 collective-permute-start
  19.0 0.0 all-to-all-done
  19.0 0.6 copy-done.7
  19.5 3.1 %pack.1 = (bf16[56,32,256]{2,1,0:T(8,128)(2,1)}, s32[88]{0:T(128)}) custom-call(s32[1]{0:T(128)} %bitcast.me_ref, s32[8,36]{1,0:T(8,128)} %bitcast.53, bf16[3,32,32,256]{3,2,1,0:T(8,128)(2,1)} %bitcast.31), custom_call_target="tpu_custom_call" | custom-call | bytes 3000000 | tf_op jit(solution)/shard_map/pack/pallas_call | solution.py:99
  22.7 4.1 %collective-permute-done = bf16[2,9,16,256]{3,2,1,0:T(8,128)(2,1)S(1)} collective-permute-done((bf16[2,9,16,256]{3,2,1,0:T(8,128)(2,1)}, bf16[2,9,16,256]{3,2,1,0:T(8,128)(2,1)S(1)}, u32[]{:S(2)}, u32[]{:S(2)}) %collective-permute-start) | collective-permute-done | bytes 147488 | tf_op jit(solution)/shard_map/ppermute | solution.py:715
  26.8 2.8 %collective-permute-start.1 = (bf16[2,9,16,256]{3,2,1,0:T(8,128)(2,1)S(1)}, bf16[2,9,16,256]{3,2,1,0:T(8,128)(2,1)S(1)}, u32[]{:S(2)}, u32[]{:S(2)}) collective-permute-start(bf16[2,9,16,256]{3,2,1,0:T(8,128)(2,1)S(1)} %bitcast.51), channel_id=1, source_target_pairs={{0,32},{8,40},{16,48},{24,56},{32,0},{40,8},{48,16},{56,24},{64,96... | collective-permute-start | bytes 442376 | tf_op jit(solution)/shard_map/ppermute | solution.py:715
  29.7 4.3 %collective-permute-done.1 = bf16[2,9,16,256]{3,2,1,0:T(8,128)(2,1)S(1)} collective-permute-done((bf16[2,9,16,256]{3,2,1,0:T(8,128)(2,1)S(1)}, bf16[2,9,16,256]{3,2,1,0:T(8,128)(2,1)S(1)}, u32[]{:S(2)}, u32[]{:S(2)}) %collective-permute-start.1) | collective-permute-done | bytes 147488 | tf_op jit(solution)/shard_map/ppermute | solution.py:715
  34.0 3.1 %collective-permute-start.2 = (bf16[2,9,16,256]{3,2,1,0:T(8,128)(2,1)S(1)}, bf16[2,9,16,256]{3,2,1,0:T(8,128)(2,1)S(1)}, u32[]{:S(2)}, u32[]{:S(2)}) collective-permute-start(bf16[2,9,16,256]{3,2,1,0:T(8,128)(2,1)S(1)} %bitcast.52), channel_id=1, source_target_pairs={{0,48},{8,56},{16,32},{24,40},{32,16},{40,24},{48,0},{56,8},{64,11... | collective-permute-start | bytes 442376 | tf_op jit(solution)/shard_map/ppermute | solution.py:715
  37.1 3.3 %collective-permute-done.2 = bf16[2,9,16,256]{3,2,1,0:T(8,128)(2,1)S(1)} collective-permute-done((bf16[2,9,16,256]{3,2,1,0:T(8,128)(2,1)S(1)}, bf16[2,9,16,256]{3,2,1,0:T(8,128)(2,1)S(1)}, u32[]{:S(2)}, u32[]{:S(2)}) %collective-permute-start.2) | collective-permute-done | bytes 147488 | tf_op jit(solution)/shard_map/ppermute | solution.py:715
  40.4 0.0 collective-permute-done.3
  40.4 0.0 collective-permute-done.4
  40.4 0.0 collective-permute-done.5
  40.5 0.0 collective-permute-done.6
  40.5 0.0 copy-start.6
  40.5 0.1 collective-permute-start.7
  40.6 5.0 %all-to-all-start.1 = ((bf16[8,7,32,256]{3,2,1,0:T(8,128)(2,1)}), bf16[8,7,32,256]{3,2,1,0:T(8,128)(2,1)S(1)}, u32[]{:S(2)}, u32[]{:S(2)}) async-start(bf16[8,7,32,256]{3,2,1,0:T(8,128)(2,1)} %bitcast.14), calls=%async_computation.1 | async-start | bytes 1835008 | tf_op jit(solution)/shard_map/all_to_all | solution.py:699
  45.6 0.6 pad_add_fusion.refs_0_.core_ref
  46.2 1.1 copy-done.8
  47.3 9.8 %conv.1 = (f32[3072,256]{1,0:T(8,128)}, bf16[2304,256]{1,0:T(8,128)(2,1)}) custom-call(s32[2]{0:T(128)} %pad_add_fusion.refs_0_.core_ref, bf16[3,32,32,256]{3,2,1,0:T(8,128)(2,1)} %bitcast.32, bf16[8,2,9,16,256]{4,3,2,1,0:T(8,128)(2,1)} %copy-done.6, bf16[8,2,9,16,256]{4,3,2,1,0:T(8,128)(2,1)} %copy-done.8), custom_call_target="tpu_custom_call" | custom-call | flops 3600000000 | bytes 7000000 | tf_op jit(solution)/shard_map/conv/pallas_call | solution.py:213
  57.1 3.5 %all-to-all-done.1 = bf16[8,7,32,256]{3,2,1,0:T(8,128)(2,1)S(1)} async-done(((bf16[8,7,32,256]{3,2,1,0:T(8,128)(2,1)}), bf16[8,7,32,256]{3,2,1,0:T(8,128)(2,1)S(1)}, u32[]{:S(2)}, u32[]{:S(2)}) %all-to-all-start.1) | async-done | bytes 917536 | tf_op jit(solution)/shard_map/all_to_all | solution.py:699
  60.6 1.0 copy-done.1
  61.6 8.3 %finish.1 = (bf16[3,32,32,256]{3,2,1,0:T(8,128)(2,1)}, f32[3072,256]{1,0:T(8,128)}, bf16[56,32,256]{2,1,0:T(8,128)(2,1)}) custom-call(s32[88]{0:T(128)} %get-tuple-element.23.routes_ref, f32[3072,256]{1,0:T(8,128)} %get-tuple-element.26.part_ref, bf16[3,32,32,256]{3,2,1,0:T(8,128)(2,1)} %bitcast.33, bf16[56,32,256]{2,1,0:T(8,128)(2,1)} %bitcast.37, ...), custom_call_target="tpu_custom_call" | custom-call | flops 200000000 | bytes 10000000 | tf_op jit(solution)/shard_map/finish/pallas_call | solution.py:297
  69.9 3.6 %all-to-all-start.2 = ((bf16[8,7,32,256]{3,2,1,0:T(8,128)(2,1)}), bf16[8,7,32,256]{3,2,1,0:T(8,128)(2,1)S(1)}, u32[]{:S(2)}, u32[]{:S(2)}) async-start(bf16[8,7,32,256]{3,2,1,0:T(8,128)(2,1)} %bitcast.43), calls=%async_computation.2 | async-start | bytes 1835008 | tf_op jit(solution)/shard_map/all_to_all | solution.py:699
  73.4 10.5 %conv_turned.1 = (f32[3072,256]{1,0:T(8,128)}, bf16[2304,256]{1,0:T(8,128)(2,1)}, bf16[2304,256]{1,0:T(8,128)(2,1)}) custom-call(s32[2]{0:T(128)} %pad_add_fusion.refs_0_.core_ref, bf16[3,32,32,256]{3,2,1,0:T(8,128)(2,1)} %get-tuple-element.29.refs_1_.field_ref, bf16[8,2,9,16,256]{4,3,2,1,0:T(8,128)(2,1)} %copy-done.6, bf16[8,2,9,16,256]{4,3,2,1,0:T(8,128)(2,1)} %copy-done.8), custom_call_target="tpu_custom_call" | custom-call | flops 3600000000 | bytes 7000000 | tf_op jit(solution)/shard_map/conv_turned/pallas_call | solution.py:213
  83.9 3.5 %all-to-all-done.2 = bf16[8,7,32,256]{3,2,1,0:T(8,128)(2,1)S(1)} async-done(((bf16[8,7,32,256]{3,2,1,0:T(8,128)(2,1)}), bf16[8,7,32,256]{3,2,1,0:T(8,128)(2,1)S(1)}, u32[]{:S(2)}, u32[]{:S(2)}) %all-to-all-start.2) | async-done | bytes 917536 | tf_op jit(solution)/shard_map/all_to_all | solution.py:699
  87.5 0.9 copy-done
  88.4 9.2 %last.1 = (bf16[3,32,32,256]{3,2,1,0:T(8,128)(2,1)}, bf16[3072,256]{1,0:T(8,128)(2,1)}, bf16[56,32,256]{2,1,0:T(8,128)(2,1)}, bf16[4,96,768]{2,1,0:T(8,128)(2,1)}) custom-call(s32[88]{0:T(128)} %get-tuple-element.23.routes_ref, f32[3072,256]{1,0:T(8,128)} %get-tuple-element.30.part_ref, bf16[3,32,32,256]{3,2,1,0:T(8,128)(2,1)} %get-tuple-element.29.refs_1_.field_ref, ...), custom_call_target="tpu_custom_call" | custom-call | flops 400000000 | bytes 12000000 | tf_op jit(solution)/shard_map/last/pallas_call | solution.py:391
  97.6 3.6 %all-to-all-start.3 = ((bf16[8,7,32,256]{3,2,1,0:T(8,128)(2,1)}), bf16[8,7,32,256]{3,2,1,0:T(8,128)(2,1)S(1)}, u32[]{:S(2)}, u32[]{:S(2)}) async-start(bf16[8,7,32,256]{3,2,1,0:T(8,128)(2,1)} %bitcast.42), calls=%async_computation.3 | async-start | bytes 1835008 | tf_op jit(solution)/shard_map/all_to_all | solution.py:699
  101.2 17.7 %second.1 = (f32[3072,256]{1,0:T(8,128)}, f32[8,9,16,256]{3,2,1,0:T(8,128)}, bf16[8,9,16,256]{3,2,1,0:T(8,128)(2,1)}) custom-call(s32[88]{0:T(128)} %get-tuple-element.23.routes_ref, s32[2]{0:T(128)} %pad_add_fusion.refs_0_.core_ref, bf16[3,32,32,256]{3,2,1,0:T(8,128)(2,1)} %get-tuple-element.29.refs_1_.field_ref, ...), custom_call_target="tpu_custom_call" | custom-call | flops 7200000000 | bytes 12000000 | tf_op jit(solution)/shard_map/second/pallas_call | solution.py:511
  118.9 0.1 collective-permute-start.9
  119.0 0.9 copy-done.2
  119.9 13.9 %first.1 = (f32[8,9,16,256]{3,2,1,0:T(8,128)}, bf16[8,9,16,256]{3,2,1,0:T(8,128)(2,1)}) custom-call(s32[88]{0:T(128)} %get-tuple-element.23.routes_ref, s32[2]{0:T(128)} %pad_add_fusion.refs_0_.core_ref, bf16[3,32,32,256]{3,2,1,0:T(8,128)(2,1)} %bitcast.34, bf16[3,32,32,256]{3,2,1,0:T(8,128)(2,1)} %bitcast.40, f32[3072,256]{1,0:T(8,128)} %get-tuple-element.37.back_ref, ...), custom_call_target="tpu_custom_call" | custom-call | flops 3600000000 | bytes 12000000 | tf_op jit(solution)/shard_map/first/pallas_call | solution.py:593
  133.8 0.5 collective-permute-start.8
  134.3 1.8 collective-permute-done.8.got1_ref
  136.2 0.8 copy-done.4
  137.0 6.0 %cut.1 = bf16[64,72,128]{2,1,0:T(8,128)(2,1)} custom-call(f32[8,9,16,256]{3,2,1,0:T(8,128)} %get-tuple-element.40.kept1_ref, bf16[8,9,16,256]{3,2,1,0:T(8,128)(2,1)} %copy-done.4, f32[8,9,16,256]{3,2,1,0:T(8,128)} %get-tuple-element.42.kept2_ref, bf16[8,9,16,256]{3,2,1,0:T(8,128)(2,1)} %copy-done.3), custom_call_target="tpu_custom_call" | custom-call | bytes 6000000 | tf_op jit(solution)/shard_map/cut/pallas_call | solution.py:640
  143.0 28.5 %all_to_all.33.in_ref = bf16[64,72,128]{2,1,0:T(8,128)(2,1)} all-to-all(bf16[64,72,128]{2,1,0:T(8,128)(2,1)} %cut.1), channel_id=1, replica_groups={{0,1,2,3,4,5,6,7,16,17,18,19,20,21,22,23,32,33,34,35,36,37,38,39,48,49,..., dimensions={0} | all-to-all | bytes 2359296 | tf_op jit(solution)/shard_map/all_to_all | solution.py:699
  171.5 2.2 %sum_all.1 = f32[8,72,128]{2,1,0:T(8,128)} custom-call(bf16[64,72,128]{2,1,0:T(8,128)(2,1)} %all_to_all.33.in_ref), custom_call_target="tpu_custom_call" | custom-call | bytes 2000000 | tf_op jit(solution)/shard_map/sum_all/pallas_call | solution.py:662
  173.6 11.7 %all_to_all.34.in_ref = f32[8,72,128]{2,1,0:T(8,128)} all-to-all(f32[8,72,128]{2,1,0:T(8,128)} %sum_all.1), channel_id=1, replica_groups=mesh['dp'=16,'space'=8] {'space'}, dimensions={0} | all-to-all | bytes 589824 | tf_op jit(solution)/shard_map/all_to_all | solution.py:699
  185.4 1.7 join.1
  (21 shorter events, 0.1 us)
Async XLA Ops:
  0.6 22.1 %copy-start.5 = (bf16[2,3,3,16,256]{4,3,2,1,0:T(8,128)(2,1)S(1)}, bf16[2,3,3,16,256]{4,3,2,1,0:T(8,128)(2,1)}, u32[]{:S(2)}) copy-start(bf16[2,3,3,16,256]{4,3,2,1,0:T(8,128)(2,1)} %param.5) | copy-start | bytes 442372
  2.1 16.9 %all-to-all-start = ((s32[8,1,36]{2,1,0:T(1,128)}), s32[8,1,36]{2,1,0:T(1,128)S(1)}, u32[]{:S(2)}, u32[]{:S(2)}) async-start(s32[8,1,36]{2,1,0:T(1,128)} %broadcast_in_dim.11), calls=%async_computation | async-start | bytes 8192 | tf_op jit(solution)/shard_map/all_to_all | solution.py:699
  7.6 32.9 %collective-permute-start.6 = (bf16[2,9,16,256]{3,2,1,0:T(8,128)(2,1)}, bf16[2,9,16,256]{3,2,1,0:T(8,128)(2,1)S(1)}, u32[]{:S(2)}, u32[]{:S(2)}) collective-permute-start(bf16[2,9,16,256]{3,2,1,0:T(8,128)(2,1)} %bitcast.45), channel_id=1, source_target_pairs={{0,112},{8,120},{16,96},{24,104},{32,80},{40,88},{48,64},{56,72},{... | collective-permute-start | bytes 442376 | tf_op jit(solution)/shard_map/ppermute | solution.py:715
  13.8 26.7 %collective-permute-start.5 = (bf16[2,9,16,256]{3,2,1,0:T(8,128)(2,1)}, bf16[2,9,16,256]{3,2,1,0:T(8,128)(2,1)S(1)}, u32[]{:S(2)}, u32[]{:S(2)}) collective-permute-start(bf16[2,9,16,256]{3,2,1,0:T(8,128)(2,1)} %bitcast.46), channel_id=1, source_target_pairs={{0,96},{8,104},{16,112},{24,120},{32,64},{40,72},{48,80},{56,88},{... | collective-permute-start | bytes 442376 | tf_op jit(solution)/shard_map/ppermute | solution.py:715
  14.0 26.4 %collective-permute-start.4 = (bf16[2,9,16,256]{3,2,1,0:T(8,128)(2,1)}, bf16[2,9,16,256]{3,2,1,0:T(8,128)(2,1)S(1)}, u32[]{:S(2)}, u32[]{:S(2)}) collective-permute-start(bf16[2,9,16,256]{3,2,1,0:T(8,128)(2,1)} %bitcast.47), channel_id=1, source_target_pairs={{0,80},{8,88},{16,64},{24,72},{32,112},{40,120},{48,96},{56,104},{... | collective-permute-start | bytes 442376 | tf_op jit(solution)/shard_map/ppermute | solution.py:715
  16.2 24.1 %collective-permute-start.3 = (bf16[2,9,16,256]{3,2,1,0:T(8,128)(2,1)}, bf16[2,9,16,256]{3,2,1,0:T(8,128)(2,1)S(1)}, u32[]{:S(2)}, u32[]{:S(2)}) collective-permute-start(bf16[2,9,16,256]{3,2,1,0:T(8,128)(2,1)} %bitcast.48), channel_id=1, source_target_pairs={{0,64},{8,72},{16,80},{24,88},{32,96},{40,104},{48,112},{56,120},{... | collective-permute-start | bytes 442376 | tf_op jit(solution)/shard_map/ppermute | solution.py:715
  17.7 9.1 %collective-permute-start = (bf16[2,9,16,256]{3,2,1,0:T(8,128)(2,1)}, bf16[2,9,16,256]{3,2,1,0:T(8,128)(2,1)S(1)}, u32[]{:S(2)}, u32[]{:S(2)}) collective-permute-start(bf16[2,9,16,256]{3,2,1,0:T(8,128)(2,1)} %bitcast.49), channel_id=1, source_target_pairs={{0,16},{8,24},{16,0},{24,8},{32,48},{40,56},{48,32},{56,40},{64,80... | collective-permute-start | bytes 442376 | tf_op jit(solution)/shard_map/ppermute | solution.py:715
  19.0 0.6 copy-start.7
  26.8 7.2 %collective-permute-start.1 = (bf16[2,9,16,256]{3,2,1,0:T(8,128)(2,1)S(1)}, bf16[2,9,16,256]{3,2,1,0:T(8,128)(2,1)S(1)}, u32[]{:S(2)}, u32[]{:S(2)}) collective-permute-start(bf16[2,9,16,256]{3,2,1,0:T(8,128)(2,1)S(1)} %bitcast.51), channel_id=1, source_target_pairs={{0,32},{8,40},{16,48},{24,56},{32,0},{40,8},{48,16},{56,24},{64,96... | collective-permute-start | bytes 442376 | tf_op jit(solution)/shard_map/ppermute | solution.py:715
  34.0 6.4 %collective-permute-start.2 = (bf16[2,9,16,256]{3,2,1,0:T(8,128)(2,1)S(1)}, bf16[2,9,16,256]{3,2,1,0:T(8,128)(2,1)S(1)}, u32[]{:S(2)}, u32[]{:S(2)}) collective-permute-start(bf16[2,9,16,256]{3,2,1,0:T(8,128)(2,1)S(1)} %bitcast.52), channel_id=1, source_target_pairs={{0,48},{8,56},{16,32},{24,40},{32,16},{40,24},{48,0},{56,8},{64,11... | collective-permute-start | bytes 442376 | tf_op jit(solution)/shard_map/ppermute | solution.py:715
  40.5 5.7 %copy-start.6 = (bf16[8,2,9,16,256]{4,3,2,1,0:T(8,128)(2,1)}, bf16[8,2,9,16,256]{4,3,2,1,0:T(8,128)(2,1)S(1)}, u32[]{:S(2)}) copy-start(bf16[8,2,9,16,256]{4,3,2,1,0:T(8,128)(2,1)S(1)} %bitcast_dynamic-update-slice_fusion.refs_2_) | copy-start | bytes 3538948
  40.5 5.7 %collective-permute-start.7 = (bf16[8,2,9,16,256]{4,3,2,1,0:T(8,128)(2,1)S(1)}, bf16[8,2,9,16,256]{4,3,2,1,0:T(8,128)(2,1)S(1)}, u32[]{:S(2)}, u32[]{:S(2)}) collective-permute-start(bf16[8,2,9,16,256]{4,3,2,1,0:T(8,128)(2,1)S(1)} %bitcast_dynamic-update-slice_fusion.refs_2_), channel_id=1, source_target_pairs={{0,8},{8,0},{16,24},{24,16},{32,40},{40,32},{48,56},{56,48},{64,72... | collective-permute-start | bytes 3538952 | tf_op jit(solution)/shard_map/ppermute | solution.py:733
  40.6 20.0 %all-to-all-start.1 = ((bf16[8,7,32,256]{3,2,1,0:T(8,128)(2,1)}), bf16[8,7,32,256]{3,2,1,0:T(8,128)(2,1)S(1)}, u32[]{:S(2)}, u32[]{:S(2)}) async-start(bf16[8,7,32,256]{3,2,1,0:T(8,128)(2,1)} %bitcast.14), calls=%async_computation.1 | async-start | bytes 1835008 | tf_op jit(solution)/shard_map/all_to_all | solution.py:699
  46.2 1.1 copy-start.8
  60.6 1.0 copy-start.1
  69.9 17.6 %all-to-all-start.2 = ((bf16[8,7,32,256]{3,2,1,0:T(8,128)(2,1)}), bf16[8,7,32,256]{3,2,1,0:T(8,128)(2,1)S(1)}, u32[]{:S(2)}, u32[]{:S(2)}) async-start(bf16[8,7,32,256]{3,2,1,0:T(8,128)(2,1)} %bitcast.43), calls=%async_computation.2 | async-start | bytes 1835008 | tf_op jit(solution)/shard_map/all_to_all | solution.py:699
  87.5 0.9 copy-start
  97.6 21.4 %all-to-all-start.3 = ((bf16[8,7,32,256]{3,2,1,0:T(8,128)(2,1)}), bf16[8,7,32,256]{3,2,1,0:T(8,128)(2,1)S(1)}, u32[]{:S(2)}, u32[]{:S(2)}) async-start(bf16[8,7,32,256]{3,2,1,0:T(8,128)(2,1)} %bitcast.42), calls=%async_computation.3 | async-start | bytes 1835008 | tf_op jit(solution)/shard_map/all_to_all | solution.py:699
  118.9 15.4 %collective-permute-start.9 = (bf16[8,9,16,256]{3,2,1,0:T(8,128)(2,1)}, bf16[8,9,16,256]{3,2,1,0:T(8,128)(2,1)S(1)}, u32[]{:S(2)}, u32[]{:S(2)}) collective-permute-start(bf16[8,9,16,256]{3,2,1,0:T(8,128)(2,1)} %get-tuple-element.43), channel_id=1, source_target_pairs={{0,8},{8,0},{16,24},{24,16},{32,40},{40,32},{48,56},{56,48},{64,72... | collective-permute-start | bytes 1769480 | tf_op jit(solution)/shard_map/ppermute | solution.py:743
  119.0 0.9 copy-start.2
  133.8 2.3 %collective-permute-start.8 = (bf16[8,9,16,256]{3,2,1,0:T(8,128)(2,1)}, bf16[8,9,16,256]{3,2,1,0:T(8,128)(2,1)S(1)}, u32[]{:S(2)}, u32[]{:S(2)}) collective-permute-start(bf16[8,9,16,256]{3,2,1,0:T(8,128)(2,1)} %get-tuple-element.41), channel_id=1, source_target_pairs={{0,8},{8,0},{16,24},{24,16},{32,40},{40,32},{48,56},{56,48},{64,72... | collective-permute-start | bytes 1769480 | tf_op jit(solution)/shard_map/ppermute | solution.py:747
  134.3 1.8 copy-start.3
  136.1 0.8 copy-start.4

commit v3 on v2

--- a/solution.py
+++ b/solution.py
@@ -196,7 +196,7 @@
             at = pl.multiple_of(c * CH + p * SIDE, SIDE)
             term = dot(wide[pl.ds(at, CH), :], kernel_ref[p * 3 * CH : (p + 1) * 3 * CH, :])
             total = term if total is None else total + term
-        part_ref[pl.ds(pl.multiple_of(c * CH, CH), CH), :] = total
+        part_ref[pl.ds(pl.multiple_of(c * CH, CH), CH), :] = total.astype(BF)
         return carry
 
     lax.fori_loop(0, CELLS // CH, chunk, 0)
@@ -205,7 +205,7 @@
 def conv(core, field, mine, theirs, layer, turned):
     pieces = pl.BlockSpec((mine.shape[0], 1, *mine.shape[2:]), lambda t: (0, layer, 0, 0, 0))
     shards = mine.shape[0] * 2
-    outs = [struct((TILES * CELLS, CH), F32), struct((9 * CH, CH), BF)]
+    outs = [struct((TILES * CELLS, CH), BF), struct((9 * CH, CH), BF)]
     specs = [per_tile(CELLS, CH), whole((9 * CH, CH))]
     if turned:
         outs.append(struct((9 * CH, CH), BF))
@@ -245,7 +245,7 @@
 
 def with_rims(part_ref, rim_part, out):
     tile = pl.program_id(0)
-    put(out, slice(None), part_ref[...])
+    put(out, slice(None), part_ref[...].astype(F32))
     for edge in range(4):
         rows = EDGE_ROWS[edge]
         add = rim_part[edge, pl.ds(pl.multiple_of(tile * SIDE, SIDE), SIDE), :]
@@ -281,7 +281,7 @@
         updated = field_ref[0, i].astype(F32) + v * s
         put(fresh, at, updated)
         state_ref[0, i] = updated.astype(BF)
-        slope_ref[at, :] = s * (1.0 + v * (1.0 - s))
+        slope_ref[at, :] = (s * (1.0 + v * (1.0 - s))).astype(BF)
         return carry
 
     lax.fori_loop(0, SIDE, one, 0, unroll=4)
@@ -299,7 +299,7 @@
         name="finish",
         out_shape=(
             struct(field.shape, BF),
-            struct(part.shape, F32),
+            struct(part.shape, BF),
             struct(got.shape, BF),
         ),
         grid=(TILES,),
@@ -574,7 +574,7 @@
 
     def two(i, carry):
         at = pl.ds(pl.multiple_of(i * SIDE, SIDE), SIDE)
-        put(fresh, at, take(fresh, at) * slope_ref[at, :])
+        put(fresh, at, take(fresh, at) * slope_ref[at, :].astype(F32))
         return carry
 
     lax.fori_loop(0, SIDE, two, 0, unroll=4)
@@ -623,15 +623,16 @@
     depth = kept1_ref.shape[2]
     run = 9 * depth // 4
     for layer, (kept_ref, got_ref) in enumerate(((kept1_ref, got1_ref), (kept2_ref, got2_ref))):
-        for tap in range(9):
-            rows[layer, tap * depth : (tap + 1) * depth, :] = kept_ref[0, tap] + got_ref[
-                0, tap
-            ].astype(F32)
-        for peer in range(8):
-            high, low = divmod(peer, 4)
-            out_ref[peer, layer * run : (layer + 1) * run, :] = rows[
-                layer, low * run : (low + 1) * run, high * 128 : (high + 1) * 128
-            ].astype(BF)
+        for pair in range(kept_ref.shape[0]):
+            for tap in range(9):
+                rows[layer, pair, tap * depth : (tap + 1) * depth, :] = kept_ref[
+                    pair, tap
+                ] + got_ref[pair, tap].astype(F32)
+            for peer in range(8):
+                high, low = divmod(peer, 4)
+                out_ref[pair * 8 + peer, layer * run : (layer + 1) * run, :] = rows[
+                    layer, pair, low * run : (low + 1) * run, high * 128 : (high + 1) * 128
+                ].astype(BF)
 
 
 def cut(kept1, got1, kept2, got2):
@@ -641,10 +642,10 @@
         cut_kernel,
         name="cut",
         out_shape=struct((pairs * 8, 2 * run, 128), BF),
-        grid=(pairs,),
-        in_specs=[per_tile(1, 9, depth, CH)] * 4,
-        out_specs=per_tile(8, 2 * run, 128),
-        scratch_shapes=[pltpu.VMEM((2, 9 * depth, CH), F32)],
+        grid=(pairs // 2,),
+        in_specs=[per_tile(2, 9, depth, CH)] * 4,
+        out_specs=per_tile(16, 2 * run, 128),
+        scratch_shapes=[pltpu.VMEM((2, 2, 9 * depth, CH), F32)],
         compiler_params=params(1),
         cost_estimate=cost(0, 6_000_000),
     )(kept1, got1, kept2, got2)
@@ -655,14 +656,14 @@
     for other in range(1, in_ref.shape[0]):
         summed = summed + in_ref[other].astype(F32)
     for peer in range(out_ref.shape[0]):
-        out_ref[peer] = summed
+        out_ref[peer] = summed.astype(BF)
 
 
 def sum_all(parts, peers):
     return pl.pallas_call(
         sum_kernel,
         name="sum_all",
-        out_shape=struct((peers, *parts.shape[1:]), F32),
+        out_shape=struct((peers, *parts.shape[1:]), BF),
         in_specs=[vmem()],
         out_specs=vmem(),
         compiler_params=params(),
@@ -680,7 +681,7 @@
             at = layer * rows_all + low * run
             out_ref[at : at + run, high * 128 : (high + 1) * 128] = in_ref[
                 peer, layer * run : (layer + 1) * run
-            ]
+            ].astype(F32)
 
 
 def join(blocks, depth):

time: 188 us -> 183 us (0.973)
  Pallas kernels: 82.5 us -> 78.2 us
    pallas_call x1, Pallas kernels: 6.04 us -> 3.98 us  [cut(): pl.pallas_call(cut_kernel, name='cut', out_shape=struct((pairs * 8, 2 * r...]
  transfers between devices with their start and end apart: 14 -> 14, of which waited for: 6 -> 6; matrix products, arithmetic and copies ran while one was open for 0% -> 0% of each run, Pallas kernels for 29% -> 30%
where the time goes in v3:
time: 183 us; the launch traced here: 182 us
  Pallas kernels  78.2 us (43%)
  blocking collectives  39.2 us (21%)
  starting transfers between devices  35.6 us (19%)
  waiting for transfers between devices  20.9 us (11%)
  local copies, waits for them, and re-layouts  6.72 us (4%)
    all_to_all x2, blocking collectives, exchange(): lax.all_to_all(value, axes, 0, 0, tiled=True, axis_index_groups=groups)  39.2 us
    pallas_call x2, Pallas kernels, conv(): pl.pallas_call(lambda *refs: conv_kernel(turned, shards, *refs), name='co...  20 us
    pallas_call x1, Pallas kernels, second(): pl.pallas_call(second_kernel, name='second', out_shape=(struct((TILES * C...  17.7 us
    all_to_all x4, starting transfers between devices, exchange(): lax.all_to_all(value, axes, 0, 0, tiled=True, axis_index_groups=groups)  17.6 us
    ppermute x7, starting transfers between devices, gather(): blocks.append(lax.ppermute(shard, 'dp', route))  17.3 us
    pallas_call x1, Pallas kernels, first(): pl.pallas_call(first_kernel, name='first', out_shape=(struct(half, F32),...  13.7 us
    ppermute x7, waiting for transfers between devices, gather(): blocks.append(lax.ppermute(shard, 'dp', route))  11.7 us
    pallas_call x1, Pallas kernels, last(): pl.pallas_call(last_kernel, name='last', out_shape=(struct(field.shape, B...  8.91 us
  transfers between devices with their start and end apart: 14, of which 6 were waited for; matrix products, arithmetic and copies ran while one was open for 0% of the time, Pallas kernels for 30%

profile of v3, /device:TPU:0, one launch (start us, length us, event | category | flops | bytes accessed | tf_op | source)
XLA Modules:
  0.0 182.1 jit_solution(9890718381511018433)
XLA Ops:
  0.6 0.0 copy-start.5
  0.6 0.8 broadcast_in_dim.10
  1.5 0.6 broadcast_in_dim.11
  2.1 5.5 %all-to-all-start = ((s32[8,1,36]{2,1,0:T(1,128)}), s32[8,1,36]{2,1,0:T(1,128)S(1)}, u32[]{:S(2)}, u32[]{:S(2)}) async-start(s32[8,1,36]{2,1,0:T(1,128)} %broadcast_in_dim.11), calls=%async_computation | async-start | bytes 8192 | tf_op jit(solution)/shard_map/all_to_all | solution.py:700
  7.6 6.2 %collective-permute-start.6 = (bf16[2,9,16,256]{3,2,1,0:T(8,128)(2,1)}, bf16[2,9,16,256]{3,2,1,0:T(8,128)(2,1)S(1)}, u32[]{:S(2)}, u32[]{:S(2)}) collective-permute-start(bf16[2,9,16,256]{3,2,1,0:T(8,128)(2,1)} %bitcast.45), channel_id=1, source_target_pairs={{0,112},{8,120},{16,96},{24,104},{32,80},{40,88},{48,64},{56,72},{... | collective-permute-start | bytes 442376 | tf_op jit(solution)/shard_map/ppermute | solution.py:716
  13.8 0.2 collective-permute-start.5
  14.0 2.3 %collective-permute-start.4 = (bf16[2,9,16,256]{3,2,1,0:T(8,128)(2,1)}, bf16[2,9,16,256]{3,2,1,0:T(8,128)(2,1)S(1)}, u32[]{:S(2)}, u32[]{:S(2)}) collective-permute-start(bf16[2,9,16,256]{3,2,1,0:T(8,128)(2,1)} %bitcast.47), channel_id=1, source_target_pairs={{0,80},{8,88},{16,64},{24,72},{32,112},{40,120},{48,96},{56,104},{... | collective-permute-start | bytes 442376 | tf_op jit(solution)/shard_map/ppermute | solution.py:716
  16.2 1.5 collective-permute-start.3
  17.7 1.3 collective-permute-start
  19.0 0.6 copy-done.7
  19.5 3.2 %pack.1 = (bf16[56,32,256]{2,1,0:T(8,128)(2,1)}, s32[88]{0:T(128)}) custom-call(s32[1]{0:T(128)} %bitcast.me_ref, s32[8,36]{1,0:T(8,128)} %bitcast.53, bf16[3,32,32,256]{3,2,1,0:T(8,128)(2,1)} %bitcast.31), custom_call_target="tpu_custom_call" | custom-call | bytes 3000000 | tf_op jit(solution)/shard_map/pack/pallas_call | solution.py:99
  22.7 4.1 %collective-permute-done = bf16[2,9,16,256]{3,2,1,0:T(8,128)(2,1)S(1)} collective-permute-done((bf16[2,9,16,256]{3,2,1,0:T(8,128)(2,1)}, bf16[2,9,16,256]{3,2,1,0:T(8,128)(2,1)S(1)}, u32[]{:S(2)}, u32[]{:S(2)}) %collective-permute-start) | collective-permute-done | bytes 147488 | tf_op jit(solution)/shard_map/ppermute | solution.py:716
  26.8 2.8 %collective-permute-start.1 = (bf16[2,9,16,256]{3,2,1,0:T(8,128)(2,1)S(1)}, bf16[2,9,16,256]{3,2,1,0:T(8,128)(2,1)S(1)}, u32[]{:S(2)}, u32[]{:S(2)}) collective-permute-start(bf16[2,9,16,256]{3,2,1,0:T(8,128)(2,1)S(1)} %bitcast.51), channel_id=1, source_target_pairs={{0,32},{8,40},{16,48},{24,56},{32,0},{40,8},{48,16},{56,24},{64,96... | collective-permute-start | bytes 442376 | tf_op jit(solution)/shard_map/ppermute | solution.py:716
  29.7 4.3 %collective-permute-done.1 = bf16[2,9,16,256]{3,2,1,0:T(8,128)(2,1)S(1)} collective-permute-done((bf16[2,9,16,256]{3,2,1,0:T(8,128)(2,1)S(1)}, bf16[2,9,16,256]{3,2,1,0:T(8,128)(2,1)S(1)}, u32[]{:S(2)}, u32[]{:S(2)}) %collective-permute-start.1) | collective-permute-done | bytes 147488 | tf_op jit(solution)/shard_map/ppermute | solution.py:716
  34.0 3.1 %collective-permute-start.2 = (bf16[2,9,16,256]{3,2,1,0:T(8,128)(2,1)S(1)}, bf16[2,9,16,256]{3,2,1,0:T(8,128)(2,1)S(1)}, u32[]{:S(2)}, u32[]{:S(2)}) collective-permute-start(bf16[2,9,16,256]{3,2,1,0:T(8,128)(2,1)S(1)} %bitcast.52), channel_id=1, source_target_pairs={{0,48},{8,56},{16,32},{24,40},{32,16},{40,24},{48,0},{56,8},{64,11... | collective-permute-start | bytes 442376 | tf_op jit(solution)/shard_map/ppermute | solution.py:716
  37.1 3.3 %collective-permute-done.2 = bf16[2,9,16,256]{3,2,1,0:T(8,128)(2,1)S(1)} collective-permute-done((bf16[2,9,16,256]{3,2,1,0:T(8,128)(2,1)S(1)}, bf16[2,9,16,256]{3,2,1,0:T(8,128)(2,1)S(1)}, u32[]{:S(2)}, u32[]{:S(2)}) %collective-permute-start.2) | collective-permute-done | bytes 147488 | tf_op jit(solution)/shard_map/ppermute | solution.py:716
  40.4 0.0 collective-permute-done.3
  40.4 0.0 collective-permute-done.4
  40.5 0.0 collective-permute-done.6
  40.5 0.1 collective-permute-start.7
  40.6 5.0 %all-to-all-start.1 = ((bf16[8,7,32,256]{3,2,1,0:T(8,128)(2,1)}), bf16[8,7,32,256]{3,2,1,0:T(8,128)(2,1)S(1)}, u32[]{:S(2)}, u32[]{:S(2)}) async-start(bf16[8,7,32,256]{3,2,1,0:T(8,128)(2,1)} %bitcast.14), calls=%async_computation.1 | async-start | bytes 1835008 | tf_op jit(solution)/shard_map/all_to_all | solution.py:700
  45.6 0.7 pad_add_fusion.refs_0_.core_ref
  46.3 0.0 collective-permute-done.7.refs_3_
  46.3 1.0 copy-done.8
  47.3 9.6 %conv.1 = (bf16[3072,256]{1,0:T(8,128)(2,1)}, bf16[2304,256]{1,0:T(8,128)(2,1)}) custom-call(s32[2]{0:T(128)} %pad_add_fusion.refs_0_.core_ref, bf16[3,32,32,256]{3,2,1,0:T(8,128)(2,1)} %bitcast.32, bf16[8,2,9,16,256]{4,3,2,1,0:T(8,128)(2,1)} %copy-done.6, bf16[8,2,9,16,256]{4,3,2,1,0:T(8,128)(2,1)} %copy-done.8), custom_call_target="tpu_custom_call" | custom-call | flops 3600000000 | bytes 7000000 | tf_op jit(solution)/shard_map/conv/pallas_call | solution.py:213
  56.9 3.7 %all-to-all-done.1 = bf16[8,7,32,256]{3,2,1,0:T(8,128)(2,1)S(1)} async-done(((bf16[8,7,32,256]{3,2,1,0:T(8,128)(2,1)}), bf16[8,7,32,256]{3,2,1,0:T(8,128)(2,1)S(1)}, u32[]{:S(2)}, u32[]{:S(2)}) %all-to-all-start.1) | async-done | bytes 917536 | tf_op jit(solution)/shard_map/all_to_all | solution.py:700
  60.6 0.9 copy-done
  61.5 7.0 %finish.1 = (bf16[3,32,32,256]{3,2,1,0:T(8,128)(2,1)}, bf16[3072,256]{1,0:T(8,128)(2,1)}, bf16[56,32,256]{2,1,0:T(8,128)(2,1)}) custom-call(s32[88]{0:T(128)} %get-tuple-element.23.routes_ref, bf16[3072,256]{1,0:T(8,128)(2,1)} %get-tuple-element.26.part_ref, bf16[3,32,32,256]{3,2,1,0:T(8,128)(2,1)} %bitcast.33, bf16[56,32,256]{2,1,0:T(8,128)(2,1)} %bitcast.35, ...), custom_call_target="tpu_custom_call" | custom-call | flops 200000000 | bytes 10000000 | tf_op jit(solution)/shard_map/finish/pallas_call | solution.py:297
  68.6 3.6 %all-to-all-start.2 = ((bf16[8,7,32,256]{3,2,1,0:T(8,128)(2,1)}), bf16[8,7,32,256]{3,2,1,0:T(8,128)(2,1)S(1)}, u32[]{:S(2)}, u32[]{:S(2)}) async-start(bf16[8,7,32,256]{3,2,1,0:T(8,128)(2,1)} %bitcast.43), calls=%async_computation.2 | async-start | bytes 1835008 | tf_op jit(solution)/shard_map/all_to_all | solution.py:700
  72.1 10.3 %conv_turned.1 = (bf16[3072,256]{1,0:T(8,128)(2,1)}, bf16[2304,256]{1,0:T(8,128)(2,1)}, bf16[2304,256]{1,0:T(8,128)(2,1)}) custom-call(s32[2]{0:T(128)} %pad_add_fusion.refs_0_.core_ref, bf16[3,32,32,256]{3,2,1,0:T(8,128)(2,1)} %get-tuple-element.29.refs_1_.field_ref, bf16[8,2,9,16,256]{4,3,2,1,0:T(8,128)(2,1)} %copy-done.6, ...), custom_call_target="tpu_custom_call" | custom-call | flops 3600000000 | bytes 7000000 | tf_op jit(solution)/shard_map/conv_turned/pallas_call | solution.py:213
  82.5 3.7 %all-to-all-done.2 = bf16[8,7,32,256]{3,2,1,0:T(8,128)(2,1)S(1)} async-done(((bf16[8,7,32,256]{3,2,1,0:T(8,128)(2,1)}), bf16[8,7,32,256]{3,2,1,0:T(8,128)(2,1)S(1)}, u32[]{:S(2)}, u32[]{:S(2)}) %all-to-all-start.2) | async-done | bytes 917536 | tf_op jit(solution)/shard_map/all_to_all | solution.py:700
  86.2 0.9 copy-done.1
  87.1 8.9 %last.1 = (bf16[3,32,32,256]{3,2,1,0:T(8,128)(2,1)}, bf16[3072,256]{1,0:T(8,128)(2,1)}, bf16[56,32,256]{2,1,0:T(8,128)(2,1)}, bf16[4,96,768]{2,1,0:T(8,128)(2,1)}) custom-call(s32[88]{0:T(128)} %get-tuple-element.23.routes_ref, bf16[3072,256]{1,0:T(8,128)(2,1)} %get-tuple-element.30.part_ref, bf16[3,32,32,256]{3,2,1,0:T(8,128)(2,1)} %get-tuple-element.29.refs_1_.field_ref, ...), custom_call_target="tpu_custom_call" | custom-call | flops 400000000 | bytes 12000000 | tf_op jit(solution)/shard_map/last/pallas_call | solution.py:391
  96.0 3.6 %all-to-all-start.3 = ((bf16[8,7,32,256]{3,2,1,0:T(8,128)(2,1)}), bf16[8,7,32,256]{3,2,1,0:T(8,128)(2,1)S(1)}, u32[]{:S(2)}, u32[]{:S(2)}) async-start(bf16[8,7,32,256]{3,2,1,0:T(8,128)(2,1)} %bitcast.42), calls=%async_computation.3 | async-start | bytes 1835008 | tf_op jit(solution)/shard_map/all_to_all | solution.py:700
  99.6 17.7 %second.1 = (f32[3072,256]{1,0:T(8,128)}, f32[8,9,16,256]{3,2,1,0:T(8,128)}, bf16[8,9,16,256]{3,2,1,0:T(8,128)(2,1)}) custom-call(s32[88]{0:T(128)} %get-tuple-element.23.routes_ref, s32[2]{0:T(128)} %pad_add_fusion.refs_0_.core_ref, bf16[3,32,32,256]{3,2,1,0:T(8,128)(2,1)} %get-tuple-element.29.refs_1_.field_ref, ...), custom_call_target="tpu_custom_call" | custom-call | flops 7200000000 | bytes 12000000 | tf_op jit(solution)/shard_map/second/pallas_call | solution.py:511
  117.3 0.1 collective-permute-start.9
  117.4 0.0 all-to-all-done.3
  117.4 0.9 copy-done.2
  118.3 13.7 %first.1 = (f32[8,9,16,256]{3,2,1,0:T(8,128)}, bf16[8,9,16,256]{3,2,1,0:T(8,128)(2,1)}) custom-call(s32[88]{0:T(128)} %get-tuple-element.23.routes_ref, s32[2]{0:T(128)} %pad_add_fusion.refs_0_.core_ref, bf16[3,32,32,256]{3,2,1,0:T(8,128)(2,1)} %bitcast.34, bf16[3,32,32,256]{3,2,1,0:T(8,128)(2,1)} %bitcast.40, f32[3072,256]{1,0:T(8,128)} %get-tuple-element.37.back_ref, ...), custom_call_target="tpu_custom_call" | custom-call | flops 3600000000 | bytes 12000000 | tf_op jit(solution)/shard_map/first/pallas_call | solution.py:593
  132.0 0.5 collective-permute-start.8
  132.5 0.0 collective-permute-done.9.got2_ref
  132.5 1.8 %collective-permute-done.8.got1_ref = bf16[8,9,16,256]{3,2,1,0:T(8,128)(2,1)S(1)} collective-permute-done((bf16[8,9,16,256]{3,2,1,0:T(8,128)(2,1)}, bf16[8,9,16,256]{3,2,1,0:T(8,128)(2,1)S(1)}, u32[]{:S(2)}, u32[]{:S(2)}) %collective-permute-start.8) | collective-permute-done | bytes 589856 | tf_op jit(solution)/shard_map/ppermute | solution.py:748
  134.3 0.8 copy-done.4
  135.1 4.0 %cut.1 = bf16[64,72,128]{2,1,0:T(8,128)(2,1)} custom-call(f32[8,9,16,256]{3,2,1,0:T(8,128)} %get-tuple-element.40.kept1_ref, bf16[8,9,16,256]{3,2,1,0:T(8,128)(2,1)} %copy-done.4, f32[8,9,16,256]{3,2,1,0:T(8,128)} %get-tuple-element.42.kept2_ref, bf16[8,9,16,256]{3,2,1,0:T(8,128)(2,1)} %copy-done.3), custom_call_target="tpu_custom_call" | custom-call | bytes 6000000 | tf_op jit(solution)/shard_map/cut/pallas_call | solution.py:641
  139.1 28.5 %all_to_all.33.in_ref = bf16[64,72,128]{2,1,0:T(8,128)(2,1)} all-to-all(bf16[64,72,128]{2,1,0:T(8,128)(2,1)} %cut.1), channel_id=1, replica_groups={{0,1,2,3,4,5,6,7,16,17,18,19,20,21,22,23,32,33,34,35,36,37,38,39,48,49,..., dimensions={0} | all-to-all | bytes 2359296 | tf_op jit(solution)/shard_map/all_to_all | solution.py:700
  167.6 2.1 %sum_all.1 = bf16[8,72,128]{2,1,0:T(8,128)(2,1)} custom-call(bf16[64,72,128]{2,1,0:T(8,128)(2,1)} %all_to_all.33.in_ref), custom_call_target="tpu_custom_call" | custom-call | bytes 2000000 | tf_op jit(solution)/shard_map/sum_all/pallas_call | solution.py:663
  169.7 10.8 %all_to_all.34.in_ref = bf16[8,72,128]{2,1,0:T(8,128)(2,1)} all-to-all(bf16[8,72,128]{2,1,0:T(8,128)(2,1)} %sum_all.1), channel_id=1, replica_groups=mesh['dp'=16,'space'=8] {'space'}, dimensions={0} | all-to-all | bytes 294912 | tf_op jit(solution)/shard_map/all_to_all | solution.py:700
  180.5 1.6 join.1
  (21 shorter events, 0.1 us)
Async XLA Ops:
  0.6 22.1 %copy-start.5 = (bf16[2,3,3,16,256]{4,3,2,1,0:T(8,128)(2,1)S(1)}, bf16[2,3,3,16,256]{4,3,2,1,0:T(8,128)(2,1)}, u32[]{:S(2)}) copy-start(bf16[2,3,3,16,256]{4,3,2,1,0:T(8,128)(2,1)} %param.5) | copy-start | bytes 442372
  2.1 16.9 %all-to-all-start = ((s32[8,1,36]{2,1,0:T(1,128)}), s32[8,1,36]{2,1,0:T(1,128)S(1)}, u32[]{:S(2)}, u32[]{:S(2)}) async-start(s32[8,1,36]{2,1,0:T(1,128)} %broadcast_in_dim.11), calls=%async_computation | async-start | bytes 8192 | tf_op jit(solution)/shard_map/all_to_all | solution.py:700
  7.6 32.9 %collective-permute-start.6 = (bf16[2,9,16,256]{3,2,1,0:T(8,128)(2,1)}, bf16[2,9,16,256]{3,2,1,0:T(8,128)(2,1)S(1)}, u32[]{:S(2)}, u32[]{:S(2)}) collective-permute-start(bf16[2,9,16,256]{3,2,1,0:T(8,128)(2,1)} %bitcast.45), channel_id=1, source_target_pairs={{0,112},{8,120},{16,96},{24,104},{32,80},{40,88},{48,64},{56,72},{... | collective-permute-start | bytes 442376 | tf_op jit(solution)/shard_map/ppermute | solution.py:716
  13.8 26.7 %collective-permute-start.5 = (bf16[2,9,16,256]{3,2,1,0:T(8,128)(2,1)}, bf16[2,9,16,256]{3,2,1,0:T(8,128)(2,1)S(1)}, u32[]{:S(2)}, u32[]{:S(2)}) collective-permute-start(bf16[2,9,16,256]{3,2,1,0:T(8,128)(2,1)} %bitcast.46), channel_id=1, source_target_pairs={{0,96},{8,104},{16,112},{24,120},{32,64},{40,72},{48,80},{56,88},{... | collective-permute-start | bytes 442376 | tf_op jit(solution)/shard_map/ppermute | solution.py:716
  14.0 26.4 %collective-permute-start.4 = (bf16[2,9,16,256]{3,2,1,0:T(8,128)(2,1)}, bf16[2,9,16,256]{3,2,1,0:T(8,128)(2,1)S(1)}, u32[]{:S(2)}, u32[]{:S(2)}) collective-permute-start(bf16[2,9,16,256]{3,2,1,0:T(8,128)(2,1)} %bitcast.47), channel_id=1, source_target_pairs={{0,80},{8,88},{16,64},{24,72},{32,112},{40,120},{48,96},{56,104},{... | collective-permute-start | bytes 442376 | tf_op jit(solution)/shard_map/ppermute | solution.py:716
  16.2 24.1 %collective-permute-start.3 = (bf16[2,9,16,256]{3,2,1,0:T(8,128)(2,1)}, bf16[2,9,16,256]{3,2,1,0:T(8,128)(2,1)S(1)}, u32[]{:S(2)}, u32[]{:S(2)}) collective-permute-start(bf16[2,9,16,256]{3,2,1,0:T(8,128)(2,1)} %bitcast.48), channel_id=1, source_target_pairs={{0,64},{8,72},{16,80},{24,88},{32,96},{40,104},{48,112},{56,120},{... | collective-permute-start | bytes 442376 | tf_op jit(solution)/shard_map/ppermute | solution.py:716
  17.7 9.1 %collective-permute-start = (bf16[2,9,16,256]{3,2,1,0:T(8,128)(2,1)}, bf16[2,9,16,256]{3,2,1,0:T(8,128)(2,1)S(1)}, u32[]{:S(2)}, u32[]{:S(2)}) collective-permute-start(bf16[2,9,16,256]{3,2,1,0:T(8,128)(2,1)} %bitcast.49), channel_id=1, source_target_pairs={{0,16},{8,24},{16,0},{24,8},{32,48},{40,56},{48,32},{56,40},{64,80... | collective-permute-start | bytes 442376 | tf_op jit(solution)/shard_map/ppermute | solution.py:716
  19.0 0.6 copy-start.7
  26.8 7.2 %collective-permute-start.1 = (bf16[2,9,16,256]{3,2,1,0:T(8,128)(2,1)S(1)}, bf16[2,9,16,256]{3,2,1,0:T(8,128)(2,1)S(1)}, u32[]{:S(2)}, u32[]{:S(2)}) collective-permute-start(bf16[2,9,16,256]{3,2,1,0:T(8,128)(2,1)S(1)} %bitcast.51), channel_id=1, source_target_pairs={{0,32},{8,40},{16,48},{24,56},{32,0},{40,8},{48,16},{56,24},{64,96... | collective-permute-start | bytes 442376 | tf_op jit(solution)/shard_map/ppermute | solution.py:716
  34.0 6.4 %collective-permute-start.2 = (bf16[2,9,16,256]{3,2,1,0:T(8,128)(2,1)S(1)}, bf16[2,9,16,256]{3,2,1,0:T(8,128)(2,1)S(1)}, u32[]{:S(2)}, u32[]{:S(2)}) collective-permute-start(bf16[2,9,16,256]{3,2,1,0:T(8,128)(2,1)S(1)} %bitcast.52), channel_id=1, source_target_pairs={{0,48},{8,56},{16,32},{24,40},{32,16},{40,24},{48,0},{56,8},{64,11... | collective-permute-start | bytes 442376 | tf_op jit(solution)/shard_map/ppermute | solution.py:716
  40.5 5.8 %copy-start.6 = (bf16[8,2,9,16,256]{4,3,2,1,0:T(8,128)(2,1)}, bf16[8,2,9,16,256]{4,3,2,1,0:T(8,128)(2,1)S(1)}, u32[]{:S(2)}) copy-start(bf16[8,2,9,16,256]{4,3,2,1,0:T(8,128)(2,1)S(1)} %bitcast_dynamic-update-slice_fusion.refs_2_) | copy-start | bytes 3538948
  40.5 5.8 %collective-permute-start.7 = (bf16[8,2,9,16,256]{4,3,2,1,0:T(8,128)(2,1)S(1)}, bf16[8,2,9,16,256]{4,3,2,1,0:T(8,128)(2,1)S(1)}, u32[]{:S(2)}, u32[]{:S(2)}) collective-permute-start(bf16[8,2,9,16,256]{4,3,2,1,0:T(8,128)(2,1)S(1)} %bitcast_dynamic-update-slice_fusion.refs_2_), channel_id=1, source_target_pairs={{0,8},{8,0},{16,24},{24,16},{32,40},{40,32},{48,56},{56,48},{64,72... | collective-permute-start | bytes 3538952 | tf_op jit(solution)/shard_map/ppermute | solution.py:734
  40.6 20.0 %all-to-all-start.1 = ((bf16[8,7,32,256]{3,2,1,0:T(8,128)(2,1)}), bf16[8,7,32,256]{3,2,1,0:T(8,128)(2,1)S(1)}, u32[]{:S(2)}, u32[]{:S(2)}) async-start(bf16[8,7,32,256]{3,2,1,0:T(8,128)(2,1)} %bitcast.14), calls=%async_computation.1 | async-start | bytes 1835008 | tf_op jit(solution)/shard_map/all_to_all | solution.py:700
  46.3 1.0 copy-start.8
  60.6 0.9 copy-start
  68.6 17.6 %all-to-all-start.2 = ((bf16[8,7,32,256]{3,2,1,0:T(8,128)(2,1)}), bf16[8,7,32,256]{3,2,1,0:T(8,128)(2,1)S(1)}, u32[]{:S(2)}, u32[]{:S(2)}) async-start(bf16[8,7,32,256]{3,2,1,0:T(8,128)(2,1)} %bitcast.43), calls=%async_computation.2 | async-start | bytes 1835008 | tf_op jit(solution)/shard_map/all_to_all | solution.py:700
  86.2 0.9 copy-start.1
  96.0 21.4 %all-to-all-start.3 = ((bf16[8,7,32,256]{3,2,1,0:T(8,128)(2,1)}), bf16[8,7,32,256]{3,2,1,0:T(8,128)(2,1)S(1)}, u32[]{:S(2)}, u32[]{:S(2)}) async-start(bf16[8,7,32,256]{3,2,1,0:T(8,128)(2,1)} %bitcast.42), calls=%async_computation.3 | async-start | bytes 1835008 | tf_op jit(solution)/shard_map/all_to_all | solution.py:700
  117.3 15.2 %collective-permute-start.9 = (bf16[8,9,16,256]{3,2,1,0:T(8,128)(2,1)}, bf16[8,9,16,256]{3,2,1,0:T(8,128)(2,1)S(1)}, u32[]{:S(2)}, u32[]{:S(2)}) collective-permute-start(bf16[8,9,16,256]{3,2,1,0:T(8,128)(2,1)} %get-tuple-element.43), channel_id=1, source_target_pairs={{0,8},{8,0},{16,24},{24,16},{32,40},{40,32},{48,56},{56,48},{64,72... | collective-permute-start | bytes 1769480 | tf_op jit(solution)/shard_map/ppermute | solution.py:744
  117.4 0.9 copy-start.2
  132.0 2.3 %collective-permute-start.8 = (bf16[8,9,16,256]{3,2,1,0:T(8,128)(2,1)}, bf16[8,9,16,256]{3,2,1,0:T(8,128)(2,1)S(1)}, u32[]{:S(2)}, u32[]{:S(2)}) collective-permute-start(bf16[8,9,16,256]{3,2,1,0:T(8,128)(2,1)} %get-tuple-element.41), channel_id=1, source_target_pairs={{0,8},{8,0},{16,24},{24,16},{32,40},{40,32},{48,56},{56,48},{64,72... | collective-permute-start | bytes 1769480 | tf_op jit(solution)/shard_map/ppermute | solution.py:748
  132.5 1.8 %copy-start.3 = (bf16[8,9,16,256]{3,2,1,0:T(8,128)(2,1)}, bf16[8,9,16,256]{3,2,1,0:T(8,128)(2,1)S(1)}, u32[]{:S(2)}) copy-start(bf16[8,9,16,256]{3,2,1,0:T(8,128)(2,1)S(1)} %collective-permute-done.9.got2_ref) | copy-start | bytes 1769476
  134.3 0.8 copy-start.4

commit v4 on v3

--- a/solution.py
+++ b/solution.py
@@ -196,7 +196,7 @@
             at = pl.multiple_of(c * CH + p * SIDE, SIDE)
             term = dot(wide[pl.ds(at, CH), :], kernel_ref[p * 3 * CH : (p + 1) * 3 * CH, :])
             total = term if total is None else total + term
-        part_ref[pl.ds(pl.multiple_of(c * CH, CH), CH), :] = total.astype(BF)
+        part_ref[pl.ds(pl.multiple_of(c * CH, CH), CH), :] = total
         return carry
 
     lax.fori_loop(0, CELLS // CH, chunk, 0)
@@ -205,7 +205,7 @@
 def conv(core, field, mine, theirs, layer, turned):
     pieces = pl.BlockSpec((mine.shape[0], 1, *mine.shape[2:]), lambda t: (0, layer, 0, 0, 0))
     shards = mine.shape[0] * 2
-    outs = [struct((TILES * CELLS, CH), BF), struct((9 * CH, CH), BF)]
+    outs = [struct((TILES * CELLS, CH), F32), struct((9 * CH, CH), BF)]
     specs = [per_tile(CELLS, CH), whole((9 * CH, CH))]
     if turned:
         outs.append(struct((9 * CH, CH), BF))
@@ -245,7 +245,7 @@
 
 def with_rims(part_ref, rim_part, out):
     tile = pl.program_id(0)
-    put(out, slice(None), part_ref[...].astype(F32))
+    put(out, slice(None), part_ref[...])
     for edge in range(4):
         rows = EDGE_ROWS[edge]
         add = rim_part[edge, pl.ds(pl.multiple_of(tile * SIDE, SIDE), SIDE), :]

time: 183 us -> 184 us (level)
  no operation moved by 1% of the time
where the time goes in v4:
time: 184 us; the launch traced here: 183 us
  Pallas kernels  79.4 us (43%)
  blocking collectives  39.2 us (21%)
  starting transfers between devices  35.6 us (19%)
  waiting for transfers between devices  20.5 us (11%)
  local copies, waits for them, and re-layouts  6.72 us (4%)
    all_to_all x2, blocking collectives, exchange(): lax.all_to_all(value, axes, 0, 0, tiled=True, axis_index_groups=groups)  39.2 us
    pallas_call x2, Pallas kernels, conv(): pl.pallas_call(lambda *refs: conv_kernel(turned, shards, *refs), name='co...  20.4 us
    pallas_call x1, Pallas kernels, second(): pl.pallas_call(second_kernel, name='second', out_shape=(struct((TILES * C...  17.7 us
    all_to_all x4, starting transfers between devices, exchange(): lax.all_to_all(value, axes, 0, 0, tiled=True, axis_index_groups=groups)  17.6 us
    ppermute x7, starting transfers between devices, gather(): blocks.append(lax.ppermute(shard, 'dp', route))  17.3 us
    pallas_call x1, Pallas kernels, first(): pl.pallas_call(first_kernel, name='first', out_shape=(struct(half, F32),...  13.7 us
    ppermute x7, waiting for transfers between devices, gather(): blocks.append(lax.ppermute(shard, 'dp', route))  11.7 us
    pallas_call x1, Pallas kernels, last(): pl.pallas_call(last_kernel, name='last', out_shape=(struct(field.shape, B...  9.24 us
  transfers between devices with their start and end apart: 14, of which 6 were waited for; matrix products, arithmetic and copies ran while one was open for 0% of the time, Pallas kernels for 30%

profile of v4, /device:TPU:0, one launch (start us, length us, event | category | flops | bytes accessed | tf_op | source)
XLA Modules:
  0.0 182.8 jit_solution(8188640226336152741)
XLA Ops:
  0.6 0.0 copy-start.5
  0.6 0.8 broadcast_in_dim.10
  1.5 0.6 broadcast_in_dim.11
  2.1 5.5 %all-to-all-start = ((s32[8,1,36]{2,1,0:T(1,128)}), s32[8,1,36]{2,1,0:T(1,128)S(1)}, u32[]{:S(2)}, u32[]{:S(2)}) async-start(s32[8,1,36]{2,1,0:T(1,128)} %broadcast_in_dim.11), calls=%async_computation | async-start | bytes 8192 | tf_op jit(solution)/shard_map/all_to_all | solution.py:700
  7.6 6.2 %collective-permute-start.6 = (bf16[2,9,16,256]{3,2,1,0:T(8,128)(2,1)}, bf16[2,9,16,256]{3,2,1,0:T(8,128)(2,1)S(1)}, u32[]{:S(2)}, u32[]{:S(2)}) collective-permute-start(bf16[2,9,16,256]{3,2,1,0:T(8,128)(2,1)} %bitcast.45), channel_id=1, source_target_pairs={{0,112},{8,120},{16,96},{24,104},{32,80},{40,88},{48,64},{56,72},{... | collective-permute-start | bytes 442376 | tf_op jit(solution)/shard_map/ppermute | solution.py:716
  13.8 0.2 collective-permute-start.5
  14.0 2.3 %collective-permute-start.4 = (bf16[2,9,16,256]{3,2,1,0:T(8,128)(2,1)}, bf16[2,9,16,256]{3,2,1,0:T(8,128)(2,1)S(1)}, u32[]{:S(2)}, u32[]{:S(2)}) collective-permute-start(bf16[2,9,16,256]{3,2,1,0:T(8,128)(2,1)} %bitcast.47), channel_id=1, source_target_pairs={{0,80},{8,88},{16,64},{24,72},{32,112},{40,120},{48,96},{56,104},{... | collective-permute-start | bytes 442376 | tf_op jit(solution)/shard_map/ppermute | solution.py:716
  16.2 1.5 collective-permute-start.3
  17.7 1.3 collective-permute-start
  19.0 0.0 all-to-all-done
  19.0 0.6 copy-done.7
  19.5 3.1 %pack.1 = (bf16[56,32,256]{2,1,0:T(8,128)(2,1)}, s32[88]{0:T(128)}) custom-call(s32[1]{0:T(128)} %bitcast.me_ref, s32[8,36]{1,0:T(8,128)} %bitcast.53, bf16[3,32,32,256]{3,2,1,0:T(8,128)(2,1)} %bitcast.31), custom_call_target="tpu_custom_call" | custom-call | bytes 3000000 | tf_op jit(solution)/shard_map/pack/pallas_call | solution.py:99
  22.7 4.1 %collective-permute-done = bf16[2,9,16,256]{3,2,1,0:T(8,128)(2,1)S(1)} collective-permute-done((bf16[2,9,16,256]{3,2,1,0:T(8,128)(2,1)}, bf16[2,9,16,256]{3,2,1,0:T(8,128)(2,1)S(1)}, u32[]{:S(2)}, u32[]{:S(2)}) %collective-permute-start) | collective-permute-done | bytes 147488 | tf_op jit(solution)/shard_map/ppermute | solution.py:716
  26.8 2.8 %collective-permute-start.1 = (bf16[2,9,16,256]{3,2,1,0:T(8,128)(2,1)S(1)}, bf16[2,9,16,256]{3,2,1,0:T(8,128)(2,1)S(1)}, u32[]{:S(2)}, u32[]{:S(2)}) collective-permute-start(bf16[2,9,16,256]{3,2,1,0:T(8,128)(2,1)S(1)} %bitcast.51), channel_id=1, source_target_pairs={{0,32},{8,40},{16,48},{24,56},{32,0},{40,8},{48,16},{56,24},{64,96... | collective-permute-start | bytes 442376 | tf_op jit(solution)/shard_map/ppermute | solution.py:716
  29.7 4.3 %collective-permute-done.1 = bf16[2,9,16,256]{3,2,1,0:T(8,128)(2,1)S(1)} collective-permute-done((bf16[2,9,16,256]{3,2,1,0:T(8,128)(2,1)S(1)}, bf16[2,9,16,256]{3,2,1,0:T(8,128)(2,1)S(1)}, u32[]{:S(2)}, u32[]{:S(2)}) %collective-permute-start.1) | collective-permute-done | bytes 147488 | tf_op jit(solution)/shard_map/ppermute | solution.py:716
  34.0 3.1 %collective-permute-start.2 = (bf16[2,9,16,256]{3,2,1,0:T(8,128)(2,1)S(1)}, bf16[2,9,16,256]{3,2,1,0:T(8,128)(2,1)S(1)}, u32[]{:S(2)}, u32[]{:S(2)}) collective-permute-start(bf16[2,9,16,256]{3,2,1,0:T(8,128)(2,1)S(1)} %bitcast.52), channel_id=1, source_target_pairs={{0,48},{8,56},{16,32},{24,40},{32,16},{40,24},{48,0},{56,8},{64,11... | collective-permute-start | bytes 442376 | tf_op jit(solution)/shard_map/ppermute | solution.py:716
  37.1 3.3 %collective-permute-done.2 = bf16[2,9,16,256]{3,2,1,0:T(8,128)(2,1)S(1)} collective-permute-done((bf16[2,9,16,256]{3,2,1,0:T(8,128)(2,1)S(1)}, bf16[2,9,16,256]{3,2,1,0:T(8,128)(2,1)S(1)}, u32[]{:S(2)}, u32[]{:S(2)}) %collective-permute-start.2) | collective-permute-done | bytes 147488 | tf_op jit(solution)/shard_map/ppermute | solution.py:716
  40.4 0.0 collective-permute-done.3
  40.4 0.0 collective-permute-done.4
  40.5 0.0 collective-permute-done.6
  40.5 0.0 copy-start.6
  40.5 0.1 collective-permute-start.7
  40.6 5.0 %all-to-all-start.1 = ((bf16[8,7,32,256]{3,2,1,0:T(8,128)(2,1)}), bf16[8,7,32,256]{3,2,1,0:T(8,128)(2,1)S(1)}, u32[]{:S(2)}, u32[]{:S(2)}) async-start(bf16[8,7,32,256]{3,2,1,0:T(8,128)(2,1)} %bitcast.14), calls=%async_computation.1 | async-start | bytes 1835008 | tf_op jit(solution)/shard_map/all_to_all | solution.py:700
  45.6 0.7 pad_add_fusion.refs_0_.core_ref
  46.3 1.0 copy-done.8
  47.3 9.9 %conv.1 = (f32[3072,256]{1,0:T(8,128)}, bf16[2304,256]{1,0:T(8,128)(2,1)}) custom-call(s32[2]{0:T(128)} %pad_add_fusion.refs_0_.core_ref, bf16[3,32,32,256]{3,2,1,0:T(8,128)(2,1)} %bitcast.32, bf16[8,2,9,16,256]{4,3,2,1,0:T(8,128)(2,1)} %copy-done.6, bf16[8,2,9,16,256]{4,3,2,1,0:T(8,128)(2,1)} %copy-done.8), custom_call_target="tpu_custom_call" | custom-call | flops 3600000000 | bytes 7000000 | tf_op jit(solution)/shard_map/conv/pallas_call | solution.py:213
  57.2 3.4 %all-to-all-done.1 = bf16[8,7,32,256]{3,2,1,0:T(8,128)(2,1)S(1)} async-done(((bf16[8,7,32,256]{3,2,1,0:T(8,128)(2,1)}), bf16[8,7,32,256]{3,2,1,0:T(8,128)(2,1)S(1)}, u32[]{:S(2)}, u32[]{:S(2)}) %all-to-all-start.1) | async-done | bytes 917536 | tf_op jit(solution)/shard_map/all_to_all | solution.py:700
  60.6 0.9 copy-done.1
  61.5 7.4 %finish.1 = (bf16[3,32,32,256]{3,2,1,0:T(8,128)(2,1)}, bf16[3072,256]{1,0:T(8,128)(2,1)}, bf16[56,32,256]{2,1,0:T(8,128)(2,1)}) custom-call(s32[88]{0:T(128)} %get-tuple-element.23.routes_ref, f32[3072,256]{1,0:T(8,128)} %get-tuple-element.26.part_ref, bf16[3,32,32,256]{3,2,1,0:T(8,128)(2,1)} %bitcast.33, bf16[56,32,256]{2,1,0:T(8,128)(2,1)} %bitcast.37, ...), custom_call_target="tpu_custom_call" | custom-call | flops 200000000 | bytes 10000000 | tf_op jit(solution)/shard_map/finish/pallas_call | solution.py:297
  68.9 3.6 %all-to-all-start.2 = ((bf16[8,7,32,256]{3,2,1,0:T(8,128)(2,1)}), bf16[8,7,32,256]{3,2,1,0:T(8,128)(2,1)S(1)}, u32[]{:S(2)}, u32[]{:S(2)}) async-start(bf16[8,7,32,256]{3,2,1,0:T(8,128)(2,1)} %bitcast.43), calls=%async_computation.2 | async-start | bytes 1835008 | tf_op jit(solution)/shard_map/all_to_all | solution.py:700
  72.5 10.5 %conv_turned.1 = (f32[3072,256]{1,0:T(8,128)}, bf16[2304,256]{1,0:T(8,128)(2,1)}, bf16[2304,256]{1,0:T(8,128)(2,1)}) custom-call(s32[2]{0:T(128)} %pad_add_fusion.refs_0_.core_ref, bf16[3,32,32,256]{3,2,1,0:T(8,128)(2,1)} %get-tuple-element.29.refs_1_.field_ref, bf16[8,2,9,16,256]{4,3,2,1,0:T(8,128)(2,1)} %copy-done.6, bf16[8,2,9,16,256]{4,3,2,1,0:T(8,128)(2,1)} %copy-done.8), custom_call_target="tpu_custom_call" | custom-call | flops 3600000000 | bytes 7000000 | tf_op jit(solution)/shard_map/conv_turned/pallas_call | solution.py:213
  83.0 3.5 %all-to-all-done.2 = bf16[8,7,32,256]{3,2,1,0:T(8,128)(2,1)S(1)} async-done(((bf16[8,7,32,256]{3,2,1,0:T(8,128)(2,1)}), bf16[8,7,32,256]{3,2,1,0:T(8,128)(2,1)S(1)}, u32[]{:S(2)}, u32[]{:S(2)}) %all-to-all-start.2) | async-done | bytes 917536 | tf_op jit(solution)/shard_map/all_to_all | solution.py:700
  86.5 0.9 copy-done
  87.5 9.2 %last.1 = (bf16[3,32,32,256]{3,2,1,0:T(8,128)(2,1)}, bf16[3072,256]{1,0:T(8,128)(2,1)}, bf16[56,32,256]{2,1,0:T(8,128)(2,1)}, bf16[4,96,768]{2,1,0:T(8,128)(2,1)}) custom-call(s32[88]{0:T(128)} %get-tuple-element.23.routes_ref, f32[3072,256]{1,0:T(8,128)} %get-tuple-element.30.part_ref, bf16[3,32,32,256]{3,2,1,0:T(8,128)(2,1)} %get-tuple-element.29.refs_1_.field_ref, ...), custom_call_target="tpu_custom_call" | custom-call | flops 400000000 | bytes 12000000 | tf_op jit(solution)/shard_map/last/pallas_call | solution.py:391
  96.7 3.6 %all-to-all-start.3 = ((bf16[8,7,32,256]{3,2,1,0:T(8,128)(2,1)}), bf16[8,7,32,256]{3,2,1,0:T(8,128)(2,1)S(1)}, u32[]{:S(2)}, u32[]{:S(2)}) async-start(bf16[8,7,32,256]{3,2,1,0:T(8,128)(2,1)} %bitcast.42), calls=%async_computation.3 | async-start | bytes 1835008 | tf_op jit(solution)/shard_map/all_to_all | solution.py:700
  100.3 17.7 %second.1 = (f32[3072,256]{1,0:T(8,128)}, f32[8,9,16,256]{3,2,1,0:T(8,128)}, bf16[8,9,16,256]{3,2,1,0:T(8,128)(2,1)}) custom-call(s32[88]{0:T(128)} %get-tuple-element.23.routes_ref, s32[2]{0:T(128)} %pad_add_fusion.refs_0_.core_ref, bf16[3,32,32,256]{3,2,1,0:T(8,128)(2,1)} %get-tuple-element.29.refs_1_.field_ref, ...), custom_call_target="tpu_custom_call" | custom-call | flops 7200000000 | bytes 12000000 | tf_op jit(solution)/shard_map/second/pallas_call | solution.py:511
  118.0 0.1 collective-permute-start.9
  118.1 0.9 copy-done.2
  119.0 13.7 %first.1 = (f32[8,9,16,256]{3,2,1,0:T(8,128)}, bf16[8,9,16,256]{3,2,1,0:T(8,128)(2,1)}) custom-call(s32[88]{0:T(128)} %get-tuple-element.23.routes_ref, s32[2]{0:T(128)} %pad_add_fusion.refs_0_.core_ref, bf16[3,32,32,256]{3,2,1,0:T(8,128)(2,1)} %bitcast.34, bf16[3,32,32,256]{3,2,1,0:T(8,128)(2,1)} %bitcast.40, f32[3072,256]{1,0:T(8,128)} %get-tuple-element.37.back_ref, ...), custom_call_target="tpu_custom_call" | custom-call | flops 3600000000 | bytes 12000000 | tf_op jit(solution)/shard_map/first/pallas_call | solution.py:593
  132.7 0.5 collective-permute-start.8
  133.2 0.0 collective-permute-done.9.got2_ref
  133.2 1.8 %collective-permute-done.8.got1_ref = bf16[8,9,16,256]{3,2,1,0:T(8,128)(2,1)S(1)} collective-permute-done((bf16[8,9,16,256]{3,2,1,0:T(8,128)(2,1)}, bf16[8,9,16,256]{3,2,1,0:T(8,128)(2,1)S(1)}, u32[]{:S(2)}, u32[]{:S(2)}) %collective-permute-start.8) | collective-permute-done | bytes 589856 | tf_op jit(solution)/shard_map/ppermute | solution.py:748
  135.0 0.8 copy-done.4
  135.8 4.0 %cut.1 = bf16[64,72,128]{2,1,0:T(8,128)(2,1)} custom-call(f32[8,9,16,256]{3,2,1,0:T(8,128)} %get-tuple-element.40.kept1_ref, bf16[8,9,16,256]{3,2,1,0:T(8,128)(2,1)} %copy-done.4, f32[8,9,16,256]{3,2,1,0:T(8,128)} %get-tuple-element.42.kept2_ref, bf16[8,9,16,256]{3,2,1,0:T(8,128)(2,1)} %copy-done.3), custom_call_target="tpu_custom_call" | custom-call | bytes 6000000 | tf_op jit(solution)/shard_map/cut/pallas_call | solution.py:641
  139.8 28.5 %all_to_all.33.in_ref = bf16[64,72,128]{2,1,0:T(8,128)(2,1)} all-to-all(bf16[64,72,128]{2,1,0:T(8,128)(2,1)} %cut.1), channel_id=1, replica_groups={{0,1,2,3,4,5,6,7,16,17,18,19,20,21,22,23,32,33,34,35,36,37,38,39,48,49,..., dimensions={0} | all-to-all | bytes 2359296 | tf_op jit(solution)/shard_map/all_to_all | solution.py:700
  168.3 2.1 %sum_all.1 = bf16[8,72,128]{2,1,0:T(8,128)(2,1)} custom-call(bf16[64,72,128]{2,1,0:T(8,128)(2,1)} %all_to_all.33.in_ref), custom_call_target="tpu_custom_call" | custom-call | bytes 2000000 | tf_op jit(solution)/shard_map/sum_all/pallas_call | solution.py:663
  170.4 10.8 %all_to_all.34.in_ref = bf16[8,72,128]{2,1,0:T(8,128)(2,1)} all-to-all(bf16[8,72,128]{2,1,0:T(8,128)(2,1)} %sum_all.1), channel_id=1, replica_groups=mesh['dp'=16,'space'=8] {'space'}, dimensions={0} | all-to-all | bytes 294912 | tf_op jit(solution)/shard_map/all_to_all | solution.py:700
  181.2 1.6 join.1
  (21 shorter events, 0.1 us)
Async XLA Ops:
  0.6 22.1 %copy-start.5 = (bf16[2,3,3,16,256]{4,3,2,1,0:T(8,128)(2,1)S(1)}, bf16[2,3,3,16,256]{4,3,2,1,0:T(8,128)(2,1)}, u32[]{:S(2)}) copy-start(bf16[2,3,3,16,256]{4,3,2,1,0:T(8,128)(2,1)} %param.5) | copy-start | bytes 442372
  2.1 16.9 %all-to-all-start = ((s32[8,1,36]{2,1,0:T(1,128)}), s32[8,1,36]{2,1,0:T(1,128)S(1)}, u32[]{:S(2)}, u32[]{:S(2)}) async-start(s32[8,1,36]{2,1,0:T(1,128)} %broadcast_in_dim.11), calls=%async_computation | async-start | bytes 8192 | tf_op jit(solution)/shard_map/all_to_all | solution.py:700
  7.6 32.9 %collective-permute-start.6 = (bf16[2,9,16,256]{3,2,1,0:T(8,128)(2,1)}, bf16[2,9,16,256]{3,2,1,0:T(8,128)(2,1)S(1)}, u32[]{:S(2)}, u32[]{:S(2)}) collective-permute-start(bf16[2,9,16,256]{3,2,1,0:T(8,128)(2,1)} %bitcast.45), channel_id=1, source_target_pairs={{0,112},{8,120},{16,96},{24,104},{32,80},{40,88},{48,64},{56,72},{... | collective-permute-start | bytes 442376 | tf_op jit(solution)/shard_map/ppermute | solution.py:716
  13.8 26.7 %collective-permute-start.5 = (bf16[2,9,16,256]{3,2,1,0:T(8,128)(2,1)}, bf16[2,9,16,256]{3,2,1,0:T(8,128)(2,1)S(1)}, u32[]{:S(2)}, u32[]{:S(2)}) collective-permute-start(bf16[2,9,16,256]{3,2,1,0:T(8,128)(2,1)} %bitcast.46), channel_id=1, source_target_pairs={{0,96},{8,104},{16,112},{24,120},{32,64},{40,72},{48,80},{56,88},{... | collective-permute-start | bytes 442376 | tf_op jit(solution)/shard_map/ppermute | solution.py:716
  14.0 26.4 %collective-permute-start.4 = (bf16[2,9,16,256]{3,2,1,0:T(8,128)(2,1)}, bf16[2,9,16,256]{3,2,1,0:T(8,128)(2,1)S(1)}, u32[]{:S(2)}, u32[]{:S(2)}) collective-permute-start(bf16[2,9,16,256]{3,2,1,0:T(8,128)(2,1)} %bitcast.47), channel_id=1, source_target_pairs={{0,80},{8,88},{16,64},{24,72},{32,112},{40,120},{48,96},{56,104},{... | collective-permute-start | bytes 442376 | tf_op jit(solution)/shard_map/ppermute | solution.py:716
  16.2 24.1 %collective-permute-start.3 = (bf16[2,9,16,256]{3,2,1,0:T(8,128)(2,1)}, bf16[2,9,16,256]{3,2,1,0:T(8,128)(2,1)S(1)}, u32[]{:S(2)}, u32[]{:S(2)}) collective-permute-start(bf16[2,9,16,256]{3,2,1,0:T(8,128)(2,1)} %bitcast.48), channel_id=1, source_target_pairs={{0,64},{8,72},{16,80},{24,88},{32,96},{40,104},{48,112},{56,120},{... | collective-permute-start | bytes 442376 | tf_op jit(solution)/shard_map/ppermute | solution.py:716
  17.7 9.1 %collective-permute-start = (bf16[2,9,16,256]{3,2,1,0:T(8,128)(2,1)}, bf16[2,9,16,256]{3,2,1,0:T(8,128)(2,1)S(1)}, u32[]{:S(2)}, u32[]{:S(2)}) collective-permute-start(bf16[2,9,16,256]{3,2,1,0:T(8,128)(2,1)} %bitcast.49), channel_id=1, source_target_pairs={{0,16},{8,24},{16,0},{24,8},{32,48},{40,56},{48,32},{56,40},{64,80... | collective-permute-start | bytes 442376 | tf_op jit(solution)/shard_map/ppermute | solution.py:716
  19.0 0.6 copy-start.7
  26.8 7.2 %collective-permute-start.1 = (bf16[2,9,16,256]{3,2,1,0:T(8,128)(2,1)S(1)}, bf16[2,9,16,256]{3,2,1,0:T(8,128)(2,1)S(1)}, u32[]{:S(2)}, u32[]{:S(2)}) collective-permute-start(bf16[2,9,16,256]{3,2,1,0:T(8,128)(2,1)S(1)} %bitcast.51), channel_id=1, source_target_pairs={{0,32},{8,40},{16,48},{24,56},{32,0},{40,8},{48,16},{56,24},{64,96... | collective-permute-start | bytes 442376 | tf_op jit(solution)/shard_map/ppermute | solution.py:716
  34.0 6.4 %collective-permute-start.2 = (bf16[2,9,16,256]{3,2,1,0:T(8,128)(2,1)S(1)}, bf16[2,9,16,256]{3,2,1,0:T(8,128)(2,1)S(1)}, u32[]{:S(2)}, u32[]{:S(2)}) collective-permute-start(bf16[2,9,16,256]{3,2,1,0:T(8,128)(2,1)S(1)} %bitcast.52), channel_id=1, source_target_pairs={{0,48},{8,56},{16,32},{24,40},{32,16},{40,24},{48,0},{56,8},{64,11... | collective-permute-start | bytes 442376 | tf_op jit(solution)/shard_map/ppermute | solution.py:716
  40.5 5.8 %copy-start.6 = (bf16[8,2,9,16,256]{4,3,2,1,0:T(8,128)(2,1)}, bf16[8,2,9,16,256]{4,3,2,1,0:T(8,128)(2,1)S(1)}, u32[]{:S(2)}) copy-start(bf16[8,2,9,16,256]{4,3,2,1,0:T(8,128)(2,1)S(1)} %bitcast_dynamic-update-slice_fusion.refs_2_) | copy-start | bytes 3538948
  40.5 5.8 %collective-permute-start.7 = (bf16[8,2,9,16,256]{4,3,2,1,0:T(8,128)(2,1)S(1)}, bf16[8,2,9,16,256]{4,3,2,1,0:T(8,128)(2,1)S(1)}, u32[]{:S(2)}, u32[]{:S(2)}) collective-permute-start(bf16[8,2,9,16,256]{4,3,2,1,0:T(8,128)(2,1)S(1)} %bitcast_dynamic-update-slice_fusion.refs_2_), channel_id=1, source_target_pairs={{0,8},{8,0},{16,24},{24,16},{32,40},{40,32},{48,56},{56,48},{64,72... | collective-permute-start | bytes 3538952 | tf_op jit(solution)/shard_map/ppermute | solution.py:734
  40.6 20.0 %all-to-all-start.1 = ((bf16[8,7,32,256]{3,2,1,0:T(8,128)(2,1)}), bf16[8,7,32,256]{3,2,1,0:T(8,128)(2,1)S(1)}, u32[]{:S(2)}, u32[]{:S(2)}) async-start(bf16[8,7,32,256]{3,2,1,0:T(8,128)(2,1)} %bitcast.14), calls=%async_computation.1 | async-start | bytes 1835008 | tf_op jit(solution)/shard_map/all_to_all | solution.py:700
  46.3 1.0 copy-start.8
  60.6 0.9 copy-start.1
  68.9 17.6 %all-to-all-start.2 = ((bf16[8,7,32,256]{3,2,1,0:T(8,128)(2,1)}), bf16[8,7,32,256]{3,2,1,0:T(8,128)(2,1)S(1)}, u32[]{:S(2)}, u32[]{:S(2)}) async-start(bf16[8,7,32,256]{3,2,1,0:T(8,128)(2,1)} %bitcast.43), calls=%async_computation.2 | async-start | bytes 1835008 | tf_op jit(solution)/shard_map/all_to_all | solution.py:700
  86.5 0.9 copy-start
  96.7 21.4 %all-to-all-start.3 = ((bf16[8,7,32,256]{3,2,1,0:T(8,128)(2,1)}), bf16[8,7,32,256]{3,2,1,0:T(8,128)(2,1)S(1)}, u32[]{:S(2)}, u32[]{:S(2)}) async-start(bf16[8,7,32,256]{3,2,1,0:T(8,128)(2,1)} %bitcast.42), calls=%async_computation.3 | async-start | bytes 1835008 | tf_op jit(solution)/shard_map/all_to_all | solution.py:700
  118.0 15.2 %collective-permute-start.9 = (bf16[8,9,16,256]{3,2,1,0:T(8,128)(2,1)}, bf16[8,9,16,256]{3,2,1,0:T(8,128)(2,1)S(1)}, u32[]{:S(2)}, u32[]{:S(2)}) collective-permute-start(bf16[8,9,16,256]{3,2,1,0:T(8,128)(2,1)} %get-tuple-element.43), channel_id=1, source_target_pairs={{0,8},{8,0},{16,24},{24,16},{32,40},{40,32},{48,56},{56,48},{64,72... | collective-permute-start | bytes 1769480 | tf_op jit(solution)/shard_map/ppermute | solution.py:744
  118.1 0.9 copy-start.2
  132.7 2.3 %collective-permute-start.8 = (bf16[8,9,16,256]{3,2,1,0:T(8,128)(2,1)}, bf16[8,9,16,256]{3,2,1,0:T(8,128)(2,1)S(1)}, u32[]{:S(2)}, u32[]{:S(2)}) collective-permute-start(bf16[8,9,16,256]{3,2,1,0:T(8,128)(2,1)} %get-tuple-element.41), channel_id=1, source_target_pairs={{0,8},{8,0},{16,24},{24,16},{32,40},{40,32},{48,56},{56,48},{64,72... | collective-permute-start | bytes 1769480 | tf_op jit(solution)/shard_map/ppermute | solution.py:748
  133.2 1.8 %copy-start.3 = (bf16[8,9,16,256]{3,2,1,0:T(8,128)(2,1)}, bf16[8,9,16,256]{3,2,1,0:T(8,128)(2,1)S(1)}, u32[]{:S(2)}) copy-start(bf16[8,9,16,256]{3,2,1,0:T(8,128)(2,1)S(1)} %collective-permute-done.9.got2_ref) | copy-start | bytes 1769476
  135.0 0.8 copy-start.4
